TPU v7x, 512 devices: a whole 4x8x8 slice. The times are simulated.
512 devices in a mesh: tile: 64 (over y_hi, x, z), win: 8 (over y_lo, core).
Axes of the slice: x: 4, y: 8 (y_hi: 2, y_lo: 4; y = y_hi * 4 + y_lo), z: 8, core: 2. Of those that a mesh axis runs over, the one named last changes fastest.
Arguments:
- syndromes: int32 [32, 256, 128], P('win', 'tile'), may hold values 0 or 1
- confidence: float32 [32, 256, 128], P('win', 'tile'), may hold values from 0.25 to 2
- embed_gain: float32 [64], replicated, may hold values from -4 to 4
- embed_bias: float32 [64], replicated, may hold values from -3 to 3
- depth_kernel: float32 [4, 64, 27], replicated, may hold values from -2 to 2
- point_weight: bfloat16 [4, 64, 64], replicated, may hold values from -0.75 to 0.75
- point_bias: float32 [4, 64], replicated, may hold values from -3 to 3
- read_weight: bfloat16 [64], replicated, may hold values from -0.375 to 0.375
Outputs:
- logits: float32 [8, 16, 256, 128], P('win', None, 'tile')
All inputs are finite; a program needn't handle non-finite values. No bound on the sum of `syndromes` on one device may be relied on, other than what follows from the above.
Results may differ from a plain program's by a relative error of at most 0.017.
Values may be sent and summed in bfloat16 or wider, within the bound.
A program may use at most 64 MiB of HBM per device.

v0:
```python
import functools

import jax
import jax.numpy as jnp
from jax import lax
from jax.experimental import pallas as pl
from jax.experimental.pallas import tpu as pltpu
from jax.sharding import PartitionSpec as P

WINDOW = 16
COMMIT = 2


def exchange_kernel(axis_names, halo, slab_ref, out_ref, held, recv_sem, send_sem, local_sem):
    tiles, wins = lax.axis_size("tile"), lax.axis_size("win")
    tile, win = lax.axis_index("tile"), lax.axis_index("win")
    pieces, rows = slab_ref.shape[0], slab_ref.shape[1]
    span = held.shape[0]

    def device(tile_index, win_index):
        place = {"tile": tile_index, "win": win_index}
        return tuple(place[name] for name in axis_names)

    mesh_ids = pl.DeviceIdType.MESH
    blank = jnp.zeros((span, halo) + held.shape[2:], held.dtype)

    @pl.when(tile == 0)
    def _():
        held[:, pl.ds(0, halo)] = blank

    @pl.when(tile == tiles - 1)
    def _():
        held[:, pl.ds(rows + halo, halo)] = blank

    neighbour_tiles = 1 + (tile > 0).astype(jnp.int32) + (tile < tiles - 1).astype(jnp.int32)
    barrier = pltpu.get_barrier_semaphore()
    for shift in (-1, 0, 1):
        for other in range(wins):
            there = tile + shift
            partner = (there >= 0) & (there < tiles)
            if shift == 0:
                partner = partner & (win != other)

            @pl.when(partner)
            def _():
                pl.semaphore_signal(barrier, 1, device_id=device(there, other), device_id_type=mesh_ids)

    pl.semaphore_wait(barrier, neighbour_tiles * wins - 1)

    parts = ((-1, 0, rows + halo, halo, 0), (0, 0, halo, rows, 1), (1, rows - halo, 0, halo, 0))
    started = []
    for piece in range(pieces):
        global_piece = win * pieces + piece
        for other in range(wins):
            offset = global_piece - other
            needed = (offset >= 0) & (offset < span)
            offset = jnp.clip(offset, 0, span - 1)
            for shift, src_row, dst_row, count, kind in parts:
                there = tile + shift
                ok = needed & (there >= 0) & (there < tiles)
                there = jnp.clip(there, 0, tiles - 1)
                src = slab_ref.at[pl.ds(piece, 1), pl.ds(src_row, count)]
                dst = held.at[pl.ds(offset, 1), pl.ds(dst_row, count)]
                if shift == 0:
                    local = ok & (win == other)
                    remote = ok & (win != other)
                    copy_local = pltpu.make_async_copy(src, dst, local_sem)

                    @pl.when(local)
                    def _():
                        copy_local.start()
                        copy_local.wait()
                else:
                    remote = ok
                copy = pltpu.make_async_remote_copy(
                    src_ref=src,
                    dst_ref=dst,
                    send_sem=send_sem.at[piece, other, shift + 1],
                    recv_sem=recv_sem.at[offset, shift + 1],
                    device_id=device(there, other),
                    device_id_type=mesh_ids,
                )

                @pl.when(remote)
                def _():
                    copy.start()

                started.append((remote, copy))

    for remote, copy in started:

        @pl.when(remote)
        def _():
            copy.wait_send()

    for step in range(span):
        source_win = (win + step) // pieces
        for shift, src_row, dst_row, count, kind in parts:
            there = tile - shift
            ok = (there >= 0) & (there < tiles)
            if shift == 0:
                ok = ok & (source_win != win)
            probe = pltpu.make_async_remote_copy(
                src_ref=slab_ref.at[pl.ds(0, 1), pl.ds(src_row, count)],
                dst_ref=held.at[pl.ds(0, 1), pl.ds(dst_row, count)],
                send_sem=send_sem.at[0, 0, shift + 1],
                recv_sem=recv_sem.at[step, shift + 1],
                device_id=device(there, win),
                device_id_type=mesh_ids,
            )

            @pl.when(ok)
            def _():
                probe.wait_recv()

    out_ref[...] = held[...]


def gather_window(signed_slab, halo, axis_names):
    rounds, rows, columns = signed_slab.shape
    pieces = rounds // COMMIT
    span = WINDOW // COMMIT
    cut = jnp.transpose(signed_slab.reshape(pieces, COMMIT, rows, columns), (0, 2, 1, 3))
    shape = (span, rows + 2 * halo, COMMIT, columns)
    held = pl.pallas_call(
        functools.partial(exchange_kernel, axis_names, halo),
        out_shape=jax.ShapeDtypeStruct(shape, signed_slab.dtype),
        in_specs=[pl.BlockSpec(memory_space=pltpu.VMEM)],
        out_specs=pl.BlockSpec(memory_space=pltpu.VMEM),
        scratch_shapes=[
            pltpu.VMEM(shape, signed_slab.dtype),
            pltpu.SemaphoreType.DMA((span, 3)),
            pltpu.SemaphoreType.DMA((pieces, lax.axis_size("win"), 3)),
            pltpu.SemaphoreType.DMA,
        ],
        compiler_params=pltpu.CompilerParams(collective_id=0, has_side_effects=True),
    )(cut)
    return jnp.transpose(held, (1, 0, 2, 3)).reshape(rows + 2 * halo, WINDOW, columns)


def gelu(value):
    return 0.5 * value * (1.0 + jnp.tanh(0.7978845608028654 * (value + 0.044715 * (value * value * value))))


def network_kernel(
    rows, halo, planes_ref, gain_ref, bias_ref, taps_ref, mix_ref, shift_ref, read_ref,
    out_ref, feats, depth,
):
    layers = taps_ref.shape[0]
    extended, rounds, columns = planes_ref.shape
    channels = gain_ref.shape[0]
    groups = channels // 8
    tiles = lax.axis_size("tile")
    first_row = lax.axis_index("tile") * rows - halo

    def inside(row):
        plane_row = first_row + row
        return (plane_row >= 0) & (plane_row < rows * tiles)

    def embed(row, carry):
        keep = inside(row)
        for t in range(rounds):
            value = planes_ref[row, pl.ds(t, 1), :] * gain_ref[...] + bias_ref[...]
            value = value.astype(jnp.bfloat16).astype(jnp.float32)
            feats[0, row, :, pl.ds(t * columns, columns)] = jnp.where(keep, value, 0.0)
        return carry

    lax.fori_loop(0, extended, embed, 0)
    lane = lax.broadcasted_iota(jnp.int32, (8, columns), 1)

    def spread(value):
        left = jnp.where(lane == 0, 0.0, pltpu.roll(value, 1, 1))
        right = jnp.where(lane == columns - 1, 0.0, pltpu.roll(value, columns - 1, 1))
        return (left, value, right)

    for layer in range(layers):
        src, dst = layer % 2, (layer + 1) % 2
        last = layer == layers - 1

        def one_row(row, carry, layer=layer, src=src, dst=dst, last=last):
            def one_group(group, inner):
                lanes8 = pl.ds(pl.multiple_of(group * 8, 8), 8)
                weights = [taps_ref[layer, tap, lanes8, :] for tap in range(27)]
                window = {}

                def load(t):
                    if t < 0 or t >= rounds:
                        return None
                    return [spread(feats[src, row - 1 + b, lanes8, pl.ds(t * columns, columns)]) for b in range(3)]

                window[-1] = None
                window[0] = load(0)
                for t in range(rounds):
                    window[t + 1] = load(t + 1)
                    total = None
                    for a in range(3):
                        held = window[t + a - 1]
                        if held is None:
                            continue
                        for b in range(3):
                            for e in range(3):
                                term = weights[9 * a + 3 * b + e] * held[b][e]
                                total = term if total is None else total + term
                    depth[lanes8, pl.ds(t * columns, columns)] = total
                    window.pop(t - 1, None)
                return inner

            lax.fori_loop(0, groups, one_group, 0)
            mixed = jnp.dot(
                mix_ref[layer], depth[...].astype(jnp.bfloat16), preferred_element_type=jnp.float32
            )
            keep = inside(row)
            sums = []
            for t in range(rounds):
                cut = pl.ds(t * columns, columns)
                activated = gelu(mixed[:, t * columns : (t + 1) * columns] + shift_ref[layer])
                value = (feats[src, row, :, cut] + activated).astype(jnp.bfloat16).astype(jnp.float32)
                value = jnp.where(keep, value, 0.0)
                if last:
                    sums.append(jnp.sum(value * read_ref[...], axis=0, keepdims=True))
                else:
                    feats[dst, row, :, cut] = value
            if last:
                out_ref[row - halo] = jnp.concatenate(sums, axis=0)
            return carry

        lax.fori_loop(layer + 1, extended - layer - 1, one_row, 0)


def run_network(planes, embed_gain, embed_bias, depth_kernel, point_weight, point_bias, read_weight, rows, halo):
    extended, rounds, columns = planes.shape
    layers, channels, _ = depth_kernel.shape
    wide = lambda v: jnp.broadcast_to(v.astype(jnp.float32)[..., None], v.shape + (columns,))
    taps = wide(jnp.transpose(depth_kernel, (0, 2, 1)))
    mix = jnp.transpose(point_weight, (0, 2, 1)).astype(jnp.bfloat16)
    vmem = pl.BlockSpec(memory_space=pltpu.VMEM)
    return pl.pallas_call(
        functools.partial(network_kernel, rows, halo),
        out_shape=jax.ShapeDtypeStruct((rows, rounds, columns), jnp.float32),
        in_specs=[vmem] * 7,
        out_specs=vmem,
        scratch_shapes=[
            pltpu.VMEM((2, extended, channels, rounds * columns), jnp.float32),
            pltpu.VMEM((channels, rounds * columns), jnp.float32),
        ],
        compiler_params=pltpu.CompilerParams(vmem_limit_bytes=56 * 1024 * 1024),
    )(planes, wide(embed_gain), wide(embed_bias), taps, mix, wide(point_bias), wide(read_weight))


def shards(
    axis_names,
    syndromes,
    confidence,
    embed_gain,
    embed_bias,
    depth_kernel,
    point_weight,
    point_bias,
    read_weight,
):
    layers = depth_kernel.shape[0]
    rows = syndromes.shape[1]
    signed_slab = ((2 * syndromes - 1).astype(jnp.float32) * confidence).astype(jnp.bfloat16)
    planes = gather_window(signed_slab, layers, axis_names).astype(jnp.float32)
    logits = run_network(
        planes, embed_gain, embed_bias, depth_kernel, point_weight, point_bias, read_weight, rows, layers
    )
    return jnp.transpose(logits, (1, 0, 2))[None]


def solution(mesh):
    placed = (P("win", "tile", None), P("win", "tile", None), P(), P(), P(), P(), P(), P())
    return jax.shard_map(
        functools.partial(shards, tuple(mesh.axis_names)), mesh=mesh, in_specs=placed, out_specs=P("win", None, "tile", None), check_vma=False
    )
```

profile of v0, /device:TPU:41, one launch (start us, length us, event | category | flops | bytes accessed | tf_op | source)
XLA Modules:
  0.0 86.9 jit_solution(16289472985808351185)
XLA Ops:
  0.0 0.0 copy-start.2
  0.0 0.0 copy-start.1
  0.0 0.0 copy-start.3
  0.0 0.0 copy-start
  0.0 0.0 copy-start.4
  0.0 0.0 copy-start.5
  0.0 0.0 copy-start.6
  0.0 0.9 %copy.15 = f32[4,27,64]{2,1,0:T(8,128)S(1)} copy(f32[4,27,64]{2,0,1:T(4,128)} %bitcast.15) | data formatting | bytes 55296 | tf_op jit(solution)/shard_map/transpose | solution.py:234
  0.9 2.3 %broadcast_in_dim.14.taps_ref = f32[4,27,64,128]{3,2,1,0:T(8,128)} broadcast(f32[4,27,64]{2,1,0:T(8,128)S(1)} %copy.15), dimensions={0,1,2} | broadcast | bytes 3566592 | tf_op jit(solution)/shard_map/broadcast_in_dim | solution.py:233
  3.2 0.0 copy-done.2
  3.2 0.0 copy-done.1
  3.2 0.6 copy.19
  3.8 19.2 %shard_map.82 = bf16[8,12,2,128]{3,2,1,0:T(2,128)(2,1)} custom-call(bf16[2,4,2,128]{3,2,1,0:T(2,128)(2,1)} %bitcast.17), custom_call_target="tpu_custom_call" | custom-call | tf_op jit(solution)/shard_map/pallas_call | solution.py:125
  23.1 0.8 convert_bitcast_fusion
  23.9 0.7 copy.14
  24.6 0.0 copy-done.3
  24.6 0.7 broadcast_in_dim.15.shift_ref
  25.3 0.0 copy-done
  25.3 0.7 copy.16
  26.0 0.0 copy-done.4
  26.1 0.7 broadcast_in_dim.12.gain_ref
  26.7 0.0 copy-done.5
  26.7 0.7 broadcast_in_dim.13.bias_ref
  27.4 0.0 copy-done.6
  27.4 0.7 broadcast_in_dim.16.read_ref
  28.1 57.4 %shard_map.83 = f32[4,16,128]{2,1,0:T(8,128)} custom-call(f32[12,16,128]{2,1,0:T(8,128)} %bitcast.12, f32[64,128]{1,0:T(8,128)} %broadcast_in_dim.12.gain_ref, f32[64,128]{1,0:T(8,128)} %broadcast_in_dim.13.bias_ref, f32[4,27,64,128]{3,2,1,0:T(8,128)} %broadcast_in_dim.14.taps_ref, bf16[4,64,64]{2,1,0:T(8,128)(2,1)} %bitcast.13, ...), custom_call_target="tpu_custom_call" | custom-call | tf_op jit(solution)/shard_map/pallas_call | solution.py:237
  85.6 1.4 %copy.17 = f32[1,16,4,128]{3,2,1,0:T(4,128)} copy(f32[1,16,4,128]{3,1,2,0:T(8,128)} %bitcast.14) | data formatting | bytes 65536 | tf_op jit(solution)/shard_map/broadcast_in_dim | solution.py:268
  (1 shorter events, 0.0 us)
Async XLA Ops:
  0.0 3.2 %copy-start.2 = (s32[4,4,128]{2,1,0:T(4,128)S(1)}, s32[4,4,128]{2,1,0:T(4,128)}, u32[]{:S(2)}) copy-start(s32[4,4,128]{2,1,0:T(4,128)} %param.8) | copy-start | bytes 24580
  0.0 3.2 %copy-start.1 = (f32[4,4,128]{2,1,0:T(4,128)S(1)}, f32[4,4,128]{2,1,0:T(4,128)}, u32[]{:S(2)}) copy-start(f32[4,4,128]{2,1,0:T(4,128)} %param.9) | copy-start | bytes 24580
  0.0 24.6 %copy-start.3 = (f32[4,64]{1,0:T(4,128)S(1)}, f32[4,64]{1,0:T(4,128)}, u32[]{:S(2)}) copy-start(f32[4,64]{1,0:T(4,128)} %param.14) | copy-start | bytes 3076
  0.0 25.3 %copy-start = (bf16[4,64,64]{2,1,0:T(8,128)(2,1)S(1)}, bf16[4,64,64]{2,1,0:T(8,128)(2,1)}, u32[]{:S(2)}) copy-start(bf16[4,64,64]{2,1,0:T(8,128)(2,1)} %param.13) | copy-start | bytes 98308
  0.0 26.0 %copy-start.4 = (f32[64]{0:T(128)S(1)}, f32[64]{0:T(128)}, u32[]{:S(2)}) copy-start(f32[64]{0:T(128)} %param.10) | copy-start | bytes 772
  0.0 26.7 %copy-start.5 = (f32[64]{0:T(128)S(1)}, f32[64]{0:T(128)}, u32[]{:S(2)}) copy-start(f32[64]{0:T(128)} %param.11) | copy-start | bytes 772
  0.0 27.4 %copy-start.6 = (bf16[64]{0:T(256)(128)(2,1)S(1)}, bf16[64]{0:T(256)(128)(2,1)}, u32[]{:S(2)}) copy-start(bf16[64]{0:T(256)(128)(2,1)} %param.15) | copy-start | bytes 388
where the time goes:
time: 87.3 us; the launch traced here: 86.9 us
  Pallas kernels  76.7 us (88%)
  local copies, waits for them, and re-layouts  9.37 us (11%)
    pallas_call x1, Pallas kernels, run_network(): pl.pallas_call(functools.partial(network_kernel, rows, halo), out_shape=j...  57.4 us
    pallas_call x1, Pallas kernels, gather_window(): pl.pallas_call(functools.partial(exchange_kernel, axis_names, halo), out_...  19.2 us
    broadcast_in_dim x5, local copies, waits for them, and re-layouts, run_network(): jnp.broadcast_to(v.astype(jnp.float32)[..., None], v.shape + (columns,))  5.07 us

commit v1 on v0

--- a/solution.py
+++ b/solution.py
@@ -142,13 +142,11 @@
     return 0.5 * value * (1.0 + jnp.tanh(0.7978845608028654 * (value + 0.044715 * (value * value * value))))
 
 
-def network_kernel(
-    rows, halo, planes_ref, gain_ref, bias_ref, taps_ref, mix_ref, shift_ref, read_ref,
-    out_ref, feats, depth,
-):
-    layers = taps_ref.shape[0]
+def network_kernel(rows, halo, layers, planes_ref, slabs_ref, mix_ref, out_ref, feats, depth):
     extended, rounds, columns = planes_ref.shape
-    channels = gain_ref.shape[0]
+    channels = slabs_ref.shape[1]
+    tail = 28 * layers
+    gain_ref, bias_ref, read_ref = slabs_ref.at[tail], slabs_ref.at[tail + 1], slabs_ref.at[tail + 2]
     groups = channels // 8
     tiles = lax.axis_size("tile")
     first_row = lax.axis_index("tile") * rows - halo
@@ -180,7 +178,7 @@
         def one_row(row, carry, layer=layer, src=src, dst=dst, last=last):
             def one_group(group, inner):
                 lanes8 = pl.ds(pl.multiple_of(group * 8, 8), 8)
-                weights = [taps_ref[layer, tap, lanes8, :] for tap in range(27)]
+                weights = [slabs_ref[27 * layer + tap, lanes8, :] for tap in range(27)]
                 window = {}
 
                 def load(t):
@@ -213,7 +211,7 @@
             sums = []
             for t in range(rounds):
                 cut = pl.ds(t * columns, columns)
-                activated = gelu(mixed[:, t * columns : (t + 1) * columns] + shift_ref[layer])
+                activated = gelu(mixed[:, t * columns : (t + 1) * columns] + slabs_ref[27 * layers + layer])
                 value = (feats[src, row, :, cut] + activated).astype(jnp.bfloat16).astype(jnp.float32)
                 value = jnp.where(keep, value, 0.0)
                 if last:
@@ -230,21 +228,30 @@
 def run_network(planes, embed_gain, embed_bias, depth_kernel, point_weight, point_bias, read_weight, rows, halo):
     extended, rounds, columns = planes.shape
     layers, channels, _ = depth_kernel.shape
-    wide = lambda v: jnp.broadcast_to(v.astype(jnp.float32)[..., None], v.shape + (columns,))
-    taps = wide(jnp.transpose(depth_kernel, (0, 2, 1)))
+    stacked = jnp.concatenate(
+        [
+            jnp.transpose(depth_kernel, (0, 2, 1)).reshape(-1, channels),
+            point_bias,
+            embed_gain[None],
+            embed_bias[None],
+            read_weight.astype(jnp.float32)[None],
+        ],
+        axis=0,
+    )
+    slabs = jnp.broadcast_to(stacked[..., None], stacked.shape + (columns,))
     mix = jnp.transpose(point_weight, (0, 2, 1)).astype(jnp.bfloat16)
     vmem = pl.BlockSpec(memory_space=pltpu.VMEM)
     return pl.pallas_call(
-        functools.partial(network_kernel, rows, halo),
+        functools.partial(network_kernel, rows, halo, layers),
         out_shape=jax.ShapeDtypeStruct((rows, rounds, columns), jnp.float32),
-        in_specs=[vmem] * 7,
+        in_specs=[vmem] * 3,
         out_specs=vmem,
         scratch_shapes=[
             pltpu.VMEM((2, extended, channels, rounds * columns), jnp.float32),
             pltpu.VMEM((channels, rounds * columns), jnp.float32),
         ],
         compiler_params=pltpu.CompilerParams(vmem_limit_bytes=56 * 1024 * 1024),
-    )(planes, wide(embed_gain), wide(embed_bias), taps, mix, wide(point_bias), wide(read_weight))
+    )(planes, slabs, mix)
 
 
 def shards(

time: 87.3 us -> 86.7 us (level)
  local copies, waits for them, and re-layouts: 9.37 us -> 8.05 us
    broadcast_in_dim x5 -> x1, local copies, waits for them, and re-layouts: 5.07 us -> 2.42 us  [run_network(): slabs = jnp.broadcast_to(stacked[..., None], stacked.shape + (columns,))]
    concatenate x0 -> x1, local copies, waits for them, and re-layouts: none -> 1.39 us  [run_network(): jnp.concatenate([jnp.transpose(depth_kernel, (0, 2, 1)).reshape(-1, chann...]
where the time goes in v1:
time: 86.7 us; the launch traced here: 86.3 us
  Pallas kernels  76.7 us (88%)
  local copies, waits for them, and re-layouts  8.05 us (9%)
  other arithmetic  1.5 us (2%)
    pallas_call x1, Pallas kernels, run_network(): pl.pallas_call(functools.partial(network_kernel, rows, halo, layers), out...  57.5 us
    pallas_call x1, Pallas kernels, gather_window(): pl.pallas_call(functools.partial(exchange_kernel, axis_names, halo), out_...  19.2 us
    broadcast_in_dim x1, local copies, waits for them, and re-layouts, run_network(): slabs = jnp.broadcast_to(stacked[..., None], stacked.shape + (columns,))  2.42 us

profile of v1, /device:TPU:41, one launch (start us, length us, event | category | flops | bytes accessed | tf_op | source)
XLA Modules:
  0.0 86.3 jit_solution(11150635905869661858)
XLA Ops:
  0.0 0.0 copy-start.2
  0.0 0.0 copy-start.1
  0.0 0.0 copy-start
  0.0 0.9 copy.14
  0.9 0.7 bitcast_convert_fusion
  1.5 1.4 %concatenate.3 = f32[115,64]{1,0:T(8,128)S(1)} concatenate(f32[108,64]{1,0:T(8,128)S(1)} %reshape.11, f32[4,64]{1,0:T(4,128)} %param.14, f32[1,64]{1,0:T(1,128)} %bitcast.23, f32[1,64]{1,0:T(1,128)} %bitcast.24, f32[1,64]{1,0:T(1,128)S(1)} %bitcast_convert_fusion), dimensions={0} | concatenate | bytes 58880 | tf_op jit(solution)/shard_map/concatenate | solution.py:231
  2.9 2.4 %broadcast_in_dim.25.slabs_ref = f32[115,64,128]{2,1,0:T(8,128)} broadcast(f32[115,64]{1,0:T(8,128)S(1)} %concatenate.3), dimensions={0,1} | broadcast | bytes 3797760 | tf_op jit(solution)/shard_map/broadcast_in_dim | solution.py:241
  5.3 0.0 copy-done.2
  5.3 0.0 copy-done.1
  5.4 0.6 copy.18
  6.0 19.2 %shard_map.82 = bf16[8,12,2,128]{3,2,1,0:T(2,128)(2,1)} custom-call(bf16[2,4,2,128]{3,2,1,0:T(2,128)(2,1)} %bitcast.22), custom_call_target="tpu_custom_call" | custom-call | tf_op jit(solution)/shard_map/pallas_call | solution.py:125
  25.2 0.8 convert_bitcast_fusion
  26.0 0.7 copy.13
  26.7 0.0 copy-done
  26.7 0.7 copy.15
  27.4 57.5 %shard_map.83 = f32[4,16,128]{2,1,0:T(8,128)} custom-call(f32[12,16,128]{2,1,0:T(8,128)} %bitcast.17, f32[115,64,128]{2,1,0:T(8,128)} %broadcast_in_dim.25.slabs_ref, bf16[4,64,64]{2,1,0:T(8,128)(2,1)} %bitcast.18), custom_call_target="tpu_custom_call" | custom-call | tf_op jit(solution)/shard_map/pallas_call | solution.py:244
  84.9 1.4 %copy.16 = f32[1,16,4,128]{3,2,1,0:T(4,128)} copy(f32[1,16,4,128]{3,1,2,0:T(8,128)} %bitcast.19) | data formatting | bytes 65536 | tf_op jit(solution)/shard_map/broadcast_in_dim | solution.py:275
  (2 shorter events, 0.0 us)
Async XLA Ops:
  0.0 5.3 %copy-start.2 = (s32[4,4,128]{2,1,0:T(4,128)S(1)}, s32[4,4,128]{2,1,0:T(4,128)}, u32[]{:S(2)}) copy-start(s32[4,4,128]{2,1,0:T(4,128)} %param.8) | copy-start | bytes 24580
  0.0 5.3 %copy-start.1 = (f32[4,4,128]{2,1,0:T(4,128)S(1)}, f32[4,4,128]{2,1,0:T(4,128)}, u32[]{:S(2)}) copy-start(f32[4,4,128]{2,1,0:T(4,128)} %param.9) | copy-start | bytes 24580
  0.0 26.7 %copy-start = (bf16[4,64,64]{2,1,0:T(8,128)(2,1)S(1)}, bf16[4,64,64]{2,1,0:T(8,128)(2,1)}, u32[]{:S(2)}) copy-start(bf16[4,64,64]{2,1,0:T(8,128)(2,1)} %param.13) | copy-start | bytes 98308

commit v2 on v1

--- a/solution.py
+++ b/solution.py
@@ -164,12 +164,9 @@
         return carry
 
     lax.fori_loop(0, extended, embed, 0)
-    lane = lax.broadcasted_iota(jnp.int32, (8, columns), 1)
 
     def spread(value):
-        left = jnp.where(lane == 0, 0.0, pltpu.roll(value, 1, 1))
-        right = jnp.where(lane == columns - 1, 0.0, pltpu.roll(value, columns - 1, 1))
-        return (left, value, right)
+        return (pltpu.roll(value, 1, 1), value, pltpu.roll(value, columns - 1, 1))
 
     for layer in range(layers):
         src, dst = layer % 2, (layer + 1) % 2
@@ -179,31 +176,25 @@
             def one_group(group, inner):
                 lanes8 = pl.ds(pl.multiple_of(group * 8, 8), 8)
                 weights = [slabs_ref[27 * layer + tap, lanes8, :] for tap in range(27)]
-                window = {}
-
-                def load(t):
-                    if t < 0 or t >= rounds:
-                        return None
-                    return [spread(feats[src, row - 1 + b, lanes8, pl.ds(t * columns, columns)]) for b in range(3)]
-
-                window[-1] = None
-                window[0] = load(0)
-                for t in range(rounds):
-                    window[t + 1] = load(t + 1)
-                    total = None
+                running = {}
+                for source in range(rounds):
+                    cut = pl.ds(source * columns, columns)
+                    held = [spread(feats[src, row - 1 + b, lanes8, cut]) for b in range(3)]
                     for a in range(3):
-                        held = window[t + a - 1]
-                        if held is None:
+                        t = source - a + 1
+                        if t < 0 or t >= rounds:
                             continue
                         for b in range(3):
                             for e in range(3):
                                 term = weights[9 * a + 3 * b + e] * held[b][e]
-                                total = term if total is None else total + term
-                    depth[lanes8, pl.ds(t * columns, columns)] = total
-                    window.pop(t - 1, None)
+                                running[t] = term if t not in running else running[t] + term
+                    done = source - 1 if source < rounds - 1 else None
+                    for t in ([done] if done is not None else [rounds - 2, rounds - 1]):
+                        if t >= 0:
+                            depth[lanes8, pl.ds(t * columns, columns)] = running.pop(t)
                 return inner
 
-            lax.fori_loop(0, groups, one_group, 0)
+            lax.fori_loop(0, groups, one_group, 0, unroll=2)
             mixed = jnp.dot(
                 mix_ref[layer], depth[...].astype(jnp.bfloat16), preferred_element_type=jnp.float32
             )
@@ -239,6 +230,11 @@
         axis=0,
     )
     slabs = jnp.broadcast_to(stacked[..., None], stacked.shape + (columns,))
+    lane = jnp.arange(columns)
+    side = jnp.arange(stacked.shape[0]) % 3
+    tap_rows = jnp.arange(stacked.shape[0]) < 27 * layers
+    cancel = tap_rows[:, None] & (((side[:, None] == 0) & (lane == 0)) | ((side[:, None] == 2) & (lane == columns - 1)))
+    slabs = jnp.where(cancel[:, None, :], 0.0, slabs)
     mix = jnp.transpose(point_weight, (0, 2, 1)).astype(jnp.bfloat16)
     vmem = pl.BlockSpec(memory_space=pltpu.VMEM)
     return pl.pallas_call(

time: 86.7 us -> 77.6 us (0.90)
  Pallas kernels: 76.7 us -> 67.2 us
  other arithmetic: 1.5 us -> 4.37 us
  local copies, waits for them, and re-layouts: 8.05 us -> 5.59 us
    pallas_call x1, Pallas kernels: 57.5 us -> 48 us  [run_network(): pl.pallas_call(functools.partial(network_kernel, rows, halo, layers), out...]
    select_n x0 -> x1, other arithmetic: none -> 2.72 us  [run_network(): slabs = jnp.where(cancel[:, None, :], 0.0, slabs)]
    broadcast_in_dim x1 -> x0, local copies, waits for them, and re-layouts: 2.42 us -> none  [run_network(): slabs = jnp.broadcast_to(stacked[..., None], stacked.shape + (columns,))]
where the time goes in v2:
time: 77.6 us; the launch traced here: 77.2 us
  Pallas kernels  67.2 us (87%)
  local copies, waits for them, and re-layouts  5.59 us (7%)
  other arithmetic  4.37 us (6%)
    pallas_call x1, Pallas kernels, run_network(): pl.pallas_call(functools.partial(network_kernel, rows, halo, layers), out...  48 us
    pallas_call x1, Pallas kernels, gather_window(): pl.pallas_call(functools.partial(exchange_kernel, axis_names, halo), out_...  19.2 us
    select_n x1, other arithmetic, run_network(): slabs = jnp.where(cancel[:, None, :], 0.0, slabs)  2.72 us

profile of v2, /device:TPU:41, one launch (start us, length us, event | category | flops | bytes accessed | tf_op | source)
XLA Modules:
  0.0 77.2 jit_solution(9197687043943601789)
XLA Ops:
  0.0 0.0 copy-start.2
  0.0 0.0 copy-start.1
  0.0 0.0 copy-start
  0.1 0.1 or_and_fusion
  0.2 0.8 %copy.14 = f32[4,27,64]{2,1,0:T(8,128)S(1)} copy(f32[4,27,64]{2,0,1:T(4,128)} %bitcast.20) | data formatting | bytes 55296 | tf_op jit(solution)/shard_map/transpose | solution.py:224
  1.0 0.7 bitcast_convert_fusion
  1.7 1.4 %concatenate.3 = f32[115,64]{1,0:T(8,128)S(1)} concatenate(f32[108,64]{1,0:T(8,128)S(1)} %reshape.97, f32[4,64]{1,0:T(4,128)} %param.14, f32[1,64]{1,0:T(1,128)} %bitcast.23, f32[1,64]{1,0:T(1,128)} %bitcast.24, f32[1,64]{1,0:T(1,128)S(1)} %bitcast_convert_fusion), dimensions={0} | concatenate | bytes 58880 | tf_op jit(solution)/shard_map/concatenate | solution.py:222
  3.1 2.7 %broadcast_select_fusion.slabs_ref = f32[115,64,128]{2,1,0:T(8,128)} fusion(f32[115,64]{1,0:T(8,128)S(1)} %concatenate.3, pred[115,128]{1,0:T(8,128)(4,1)S(1)} %or_and_fusion), kind=kLoop, calls=%fused_computation | loop fusion | flops 942080 | bytes 3812480 | tf_op jit(solution)/shard_map/jit(_where)/select_n | solution.py:237
  5.8 0.0 copy-done.2
  5.8 0.0 copy-done.1
  5.8 0.6 copy.18
  6.4 19.2 %shard_map.82 = bf16[8,12,2,128]{3,2,1,0:T(2,128)(2,1)} custom-call(bf16[2,4,2,128]{3,2,1,0:T(2,128)(2,1)} %bitcast.22), custom_call_target="tpu_custom_call" | custom-call | tf_op jit(solution)/shard_map/pallas_call | solution.py:125
  25.6 0.8 %convert_bitcast_fusion = f32[12,8,2,128]{3,2,0,1:T(2,128)S(1)} fusion(bf16[8,12,2,128]{3,2,1,0:T(2,128)(2,1)} %shard_map.82), kind=kLoop, calls=%fused_computation.1 | loop fusion | flops 24576 | bytes 147456 | tf_op jit(solution)/shard_map/convert_element_type | solution.py:267
  26.5 0.7 copy.13
  27.1 0.0 copy-done
  27.1 0.7 copy.15
  27.9 48.0 %shard_map.83 = f32[4,16,128]{2,1,0:T(8,128)} custom-call(f32[12,16,128]{2,1,0:T(8,128)} %bitcast.17, f32[115,64,128]{2,1,0:T(8,128)} %broadcast_select_fusion.slabs_ref, bf16[4,64,64]{2,1,0:T(8,128)(2,1)} %bitcast.18), custom_call_target="tpu_custom_call" | custom-call | tf_op jit(solution)/shard_map/pallas_call | solution.py:240
  75.8 1.4 %copy.16 = f32[1,16,4,128]{3,2,1,0:T(4,128)} copy(f32[1,16,4,128]{3,1,2,0:T(8,128)} %bitcast.19) | data formatting | bytes 65536 | tf_op jit(solution)/shard_map/broadcast_in_dim | solution.py:271
  (5 shorter events, 0.0 us)
Async XLA Ops:
  0.0 5.8 %copy-start.2 = (s32[4,4,128]{2,1,0:T(4,128)S(1)}, s32[4,4,128]{2,1,0:T(4,128)}, u32[]{:S(2)}) copy-start(s32[4,4,128]{2,1,0:T(4,128)} %param.8) | copy-start | bytes 24580
  0.0 5.8 %copy-start.1 = (f32[4,4,128]{2,1,0:T(4,128)S(1)}, f32[4,4,128]{2,1,0:T(4,128)}, u32[]{:S(2)}) copy-start(f32[4,4,128]{2,1,0:T(4,128)} %param.9) | copy-start | bytes 24580
  0.0 27.1 %copy-start = (bf16[4,64,64]{2,1,0:T(8,128)(2,1)S(1)}, bf16[4,64,64]{2,1,0:T(8,128)(2,1)}, u32[]{:S(2)}) copy-start(bf16[4,64,64]{2,1,0:T(8,128)(2,1)} %param.13) | copy-start | bytes 98308

commit v3 on v2

--- a/solution.py
+++ b/solution.py
@@ -194,7 +194,7 @@
                             depth[lanes8, pl.ds(t * columns, columns)] = running.pop(t)
                 return inner
 
-            lax.fori_loop(0, groups, one_group, 0, unroll=2)
+            lax.fori_loop(0, groups, one_group, 0, unroll=4)
             mixed = jnp.dot(
                 mix_ref[layer], depth[...].astype(jnp.bfloat16), preferred_element_type=jnp.float32
             )

time: 77.6 us -> 72.6 us (0.936)
  Pallas kernels: 67.2 us -> 62.2 us
    pallas_call x1, Pallas kernels: 48 us -> 43 us  [run_network(): pl.pallas_call(functools.partial(network_kernel, rows, halo, layers), out...]
where the time goes in v3:
time: 72.6 us; the launch traced here: 72.2 us
  Pallas kernels  62.2 us (86%)
  local copies, waits for them, and re-layouts  5.59 us (8%)
  other arithmetic  4.37 us (6%)
    pallas_call x1, Pallas kernels, run_network(): pl.pallas_call(functools.partial(network_kernel, rows, halo, layers), out...  43 us
    pallas_call x1, Pallas kernels, gather_window(): pl.pallas_call(functools.partial(exchange_kernel, axis_names, halo), out_...  19.2 us
    select_n x1, other arithmetic, run_network(): slabs = jnp.where(cancel[:, None, :], 0.0, slabs)  2.72 us

profile of v3, /device:TPU:41, one launch (start us, length us, event | category | flops | bytes accessed | tf_op | source)
XLA Modules:
  0.0 72.2 jit_solution(13635347078619142457)
XLA Ops:
  0.0 0.0 copy-start.2
  0.0 0.0 copy-start.1
  0.0 0.0 copy-start
  0.1 0.1 or_and_fusion
  0.2 0.8 %copy.14 = f32[4,27,64]{2,1,0:T(8,128)S(1)} copy(f32[4,27,64]{2,0,1:T(4,128)} %bitcast.20) | data formatting | bytes 55296 | tf_op jit(solution)/shard_map/transpose | solution.py:224
  1.0 0.7 bitcast_convert_fusion
  1.7 1.4 %concatenate.3 = f32[115,64]{1,0:T(8,128)S(1)} concatenate(f32[108,64]{1,0:T(8,128)S(1)} %reshape.97, f32[4,64]{1,0:T(4,128)} %param.14, f32[1,64]{1,0:T(1,128)} %bitcast.23, f32[1,64]{1,0:T(1,128)} %bitcast.24, f32[1,64]{1,0:T(1,128)S(1)} %bitcast_convert_fusion), dimensions={0} | concatenate | bytes 58880 | tf_op jit(solution)/shard_map/concatenate | solution.py:222
  3.1 2.7 %broadcast_select_fusion.slabs_ref = f32[115,64,128]{2,1,0:T(8,128)} fusion(f32[115,64]{1,0:T(8,128)S(1)} %concatenate.3, pred[115,128]{1,0:T(8,128)(4,1)S(1)} %or_and_fusion), kind=kLoop, calls=%fused_computation | loop fusion | flops 942080 | bytes 3812480 | tf_op jit(solution)/shard_map/jit(_where)/select_n | solution.py:237
  5.8 0.0 copy-done.2
  5.8 0.0 copy-done.1
  5.8 0.6 copy.18
  6.4 19.2 %shard_map.82 = bf16[8,12,2,128]{3,2,1,0:T(2,128)(2,1)} custom-call(bf16[2,4,2,128]{3,2,1,0:T(2,128)(2,1)} %bitcast.22), custom_call_target="tpu_custom_call" | custom-call | tf_op jit(solution)/shard_map/pallas_call | solution.py:125
  25.6 0.8 %convert_bitcast_fusion = f32[12,8,2,128]{3,2,0,1:T(2,128)S(1)} fusion(bf16[8,12,2,128]{3,2,1,0:T(2,128)(2,1)} %shard_map.82), kind=kLoop, calls=%fused_computation.1 | loop fusion | flops 24576 | bytes 147456 | tf_op jit(solution)/shard_map/convert_element_type | solution.py:267
  26.5 0.7 copy.13
  27.1 0.0 copy-done
  27.1 0.7 copy.15
  27.9 43.0 %shard_map.83 = f32[4,16,128]{2,1,0:T(8,128)} custom-call(f32[12,16,128]{2,1,0:T(8,128)} %bitcast.17, f32[115,64,128]{2,1,0:T(8,128)} %broadcast_select_fusion.slabs_ref, bf16[4,64,64]{2,1,0:T(8,128)(2,1)} %bitcast.18), custom_call_target="tpu_custom_call" | custom-call | tf_op jit(solution)/shard_map/pallas_call | solution.py:240
  70.9 1.4 %copy.16 = f32[1,16,4,128]{3,2,1,0:T(4,128)} copy(f32[1,16,4,128]{3,1,2,0:T(8,128)} %bitcast.19) | data formatting | bytes 65536 | tf_op jit(solution)/shard_map/broadcast_in_dim | solution.py:271
  (5 shorter events, 0.0 us)
Async XLA Ops:
  0.0 5.8 %copy-start.2 = (s32[4,4,128]{2,1,0:T(4,128)S(1)}, s32[4,4,128]{2,1,0:T(4,128)}, u32[]{:S(2)}) copy-start(s32[4,4,128]{2,1,0:T(4,128)} %param.8) | copy-start | bytes 24580
  0.0 5.8 %copy-start.1 = (f32[4,4,128]{2,1,0:T(4,128)S(1)}, f32[4,4,128]{2,1,0:T(4,128)}, u32[]{:S(2)}) copy-start(f32[4,4,128]{2,1,0:T(4,128)} %param.9) | copy-start | bytes 24580
  0.0 27.1 %copy-start = (bf16[4,64,64]{2,1,0:T(8,128)(2,1)S(1)}, bf16[4,64,64]{2,1,0:T(8,128)(2,1)}, u32[]{:S(2)}) copy-start(bf16[4,64,64]{2,1,0:T(8,128)(2,1)} %param.13) | copy-start | bytes 98308

commit v4 on v3

--- a/solution.py
+++ b/solution.py
@@ -135,7 +135,7 @@
         ],
         compiler_params=pltpu.CompilerParams(collective_id=0, has_side_effects=True),
     )(cut)
-    return jnp.transpose(held, (1, 0, 2, 3)).reshape(rows + 2 * halo, WINDOW, columns)
+    return held
 
 
 def gelu(value):
@@ -143,7 +143,8 @@
 
 
 def network_kernel(rows, halo, layers, planes_ref, slabs_ref, mix_ref, out_ref, feats, depth):
-    extended, rounds, columns = planes_ref.shape
+    span, extended, commit, columns = planes_ref.shape
+    rounds = span * commit
     channels = slabs_ref.shape[1]
     tail = 28 * layers
     gain_ref, bias_ref, read_ref = slabs_ref.at[tail], slabs_ref.at[tail + 1], slabs_ref.at[tail + 2]
@@ -158,7 +159,8 @@
     def embed(row, carry):
         keep = inside(row)
         for t in range(rounds):
-            value = planes_ref[row, pl.ds(t, 1), :] * gain_ref[...] + bias_ref[...]
+            plane = planes_ref[t // commit, row, pl.ds(t % commit, 1), :].astype(jnp.float32)
+            value = plane * gain_ref[...] + bias_ref[...]
             value = value.astype(jnp.bfloat16).astype(jnp.float32)
             feats[0, row, :, pl.ds(t * columns, columns)] = jnp.where(keep, value, 0.0)
         return carry
@@ -194,7 +196,7 @@
                             depth[lanes8, pl.ds(t * columns, columns)] = running.pop(t)
                 return inner
 
-            lax.fori_loop(0, groups, one_group, 0, unroll=4)
+            lax.fori_loop(0, groups, one_group, 0, unroll=8)
             mixed = jnp.dot(
                 mix_ref[layer], depth[...].astype(jnp.bfloat16), preferred_element_type=jnp.float32
             )
@@ -217,7 +219,8 @@
 
 
 def run_network(planes, embed_gain, embed_bias, depth_kernel, point_weight, point_bias, read_weight, rows, halo):
-    extended, rounds, columns = planes.shape
+    span, extended, commit, columns = planes.shape
+    rounds = span * commit
     layers, channels, _ = depth_kernel.shape
     stacked = jnp.concatenate(
         [
@@ -264,7 +267,7 @@
     layers = depth_kernel.shape[0]
     rows = syndromes.shape[1]
     signed_slab = ((2 * syndromes - 1).astype(jnp.float32) * confidence).astype(jnp.bfloat16)
-    planes = gather_window(signed_slab, layers, axis_names).astype(jnp.float32)
+    planes = gather_window(signed_slab, layers, axis_names)
     logits = run_network(
         planes, embed_gain, embed_bias, depth_kernel, point_weight, point_bias, read_weight, rows, layers
     )

time: 72.6 us -> 66.8 us (0.920)
  Pallas kernels: 62.2 us -> 58 us
  other arithmetic: 4.37 us -> 3.53 us
    pallas_call x1, Pallas kernels: 43 us -> 38.8 us  [run_network(): pl.pallas_call(functools.partial(network_kernel, rows, halo, layers), out...]
    convert_element_type x1 -> x0, other arithmetic: 0.83 us -> none  [shards(): planes = gather_window(signed_slab, layers, axis_names).astype(jnp.float32)]
where the time goes in v4:
time: 66.8 us; the launch traced here: 66.5 us
  Pallas kernels  58 us (87%)
  local copies, waits for them, and re-layouts  4.92 us (7%)
  other arithmetic  3.53 us (5%)
    pallas_call x1, Pallas kernels, run_network(): pl.pallas_call(functools.partial(network_kernel, rows, halo, layers), out...  38.8 us
    pallas_call x1, Pallas kernels, gather_window(): pl.pallas_call(functools.partial(exchange_kernel, axis_names, halo), out_...  19.2 us
    select_n x1, other arithmetic, run_network(): slabs = jnp.where(cancel[:, None, :], 0.0, slabs)  2.72 us
    concatenate x1, local copies, waits for them, and re-layouts, run_network(): jnp.concatenate([jnp.transpose(depth_kernel, (0, 2, 1)).reshape(-1, chann...  1.39 us
    broadcast_in_dim x1, local copies, waits for them, and re-layouts, shards(): return jnp.transpose(logits, (1, 0, 2))[None]  1.39 us

profile of v4, /device:TPU:41, one launch (start us, length us, event | category | flops | bytes accessed | tf_op | source)
XLA Modules:
  0.0 66.5 jit_solution(15734744468797897572)
XLA Ops:
  0.0 0.0 copy-start
  0.0 0.0 copy-start.2
  0.0 0.0 copy-start.1
  0.1 0.1 or_and_fusion
  0.2 0.8 %copy.12 = f32[4,27,64]{2,1,0:T(8,128)S(1)} copy(f32[4,27,64]{2,0,1:T(4,128)} %bitcast.16) | data formatting | bytes 55296 | tf_op jit(solution)/shard_map/transpose | solution.py:227
  1.0 0.7 bitcast_convert_fusion
  1.7 1.4 %concatenate.3 = f32[115,64]{1,0:T(8,128)S(1)} concatenate(f32[108,64]{1,0:T(8,128)S(1)} %reshape.94, f32[4,64]{1,0:T(4,128)} %param.14, f32[1,64]{1,0:T(1,128)} %bitcast.19, f32[1,64]{1,0:T(1,128)} %bitcast.20, f32[1,64]{1,0:T(1,128)S(1)} %bitcast_convert_fusion), dimensions={0} | concatenate | bytes 58880 | tf_op jit(solution)/shard_map/concatenate | solution.py:225
  3.1 2.7 %broadcast_select_fusion.slabs_ref = f32[115,64,128]{2,1,0:T(8,128)} fusion(f32[115,64]{1,0:T(8,128)S(1)} %concatenate.3, pred[115,128]{1,0:T(8,128)(4,1)S(1)} %or_and_fusion), kind=kLoop, calls=%fused_computation | loop fusion | flops 942080 | bytes 3812480 | tf_op jit(solution)/shard_map/jit(_where)/select_n | solution.py:240
  5.8 0.0 copy-done
  5.8 0.7 %copy.13 = bf16[4,64,64]{1,2,0:T(8,128)(2,1)} copy(bf16[4,64,64]{2,1,0:T(8,128)(2,1)S(1)} %copy-done) | data formatting | bytes 65536 | tf_op args[5]
  6.5 0.0 copy-done.2
  6.5 0.0 copy-done.1
  6.5 0.6 copy.16
  7.1 19.2 %shard_map.82.planes_ref = bf16[8,12,2,128]{3,2,1,0:T(2,128)(2,1)} custom-call(bf16[2,4,2,128]{3,2,1,0:T(2,128)(2,1)} %bitcast.18), custom_call_target="tpu_custom_call" | custom-call | tf_op jit(solution)/shard_map/pallas_call | solution.py:125
  26.4 38.8 %shard_map.83 = f32[4,16,128]{2,1,0:T(8,128)} custom-call(bf16[8,12,2,128]{3,2,1,0:T(2,128)(2,1)} %shard_map.82.planes_ref, f32[115,64,128]{2,1,0:T(8,128)} %broadcast_select_fusion.slabs_ref, bf16[4,64,64]{2,1,0:T(8,128)(2,1)} %bitcast.14), custom_call_target="tpu_custom_call" | custom-call | tf_op jit(solution)/shard_map/pallas_call | solution.py:243
  65.2 1.4 %copy.14 = f32[1,16,4,128]{3,2,1,0:T(4,128)} copy(f32[1,16,4,128]{3,1,2,0:T(8,128)} %bitcast.15) | data formatting | bytes 65536 | tf_op jit(solution)/shard_map/broadcast_in_dim | solution.py:274
  (5 shorter events, 0.0 us)
Async XLA Ops:
  0.0 5.8 %copy-start = (bf16[4,64,64]{2,1,0:T(8,128)(2,1)S(1)}, bf16[4,64,64]{2,1,0:T(8,128)(2,1)}, u32[]{:S(2)}) copy-start(bf16[4,64,64]{2,1,0:T(8,128)(2,1)} %param.13) | copy-start | bytes 98308
  0.0 6.5 %copy-start.2 = (s32[4,4,128]{2,1,0:T(4,128)S(1)}, s32[4,4,128]{2,1,0:T(4,128)}, u32[]{:S(2)}) copy-start(s32[4,4,128]{2,1,0:T(4,128)} %param.8) | copy-start | bytes 24580
  0.0 6.5 %copy-start.1 = (f32[4,4,128]{2,1,0:T(4,128)S(1)}, f32[4,4,128]{2,1,0:T(4,128)}, u32[]{:S(2)}) copy-start(f32[4,4,128]{2,1,0:T(4,128)} %param.9) | copy-start | bytes 24580

commit v5 on v4

--- a/solution.py
+++ b/solution.py
@@ -142,10 +142,18 @@
     return 0.5 * value * (1.0 + jnp.tanh(0.7978845608028654 * (value + 0.044715 * (value * value * value))))
 
 
-def network_kernel(rows, halo, layers, planes_ref, slabs_ref, mix_ref, out_ref, feats, depth):
+def network_kernel(rows, halo, layers, planes_ref, compact_ref, mix_ref, out_ref, feats, depth, slabs_ref):
     span, extended, commit, columns = planes_ref.shape
     rounds = span * commit
     channels = slabs_ref.shape[1]
+    lane = lax.broadcasted_iota(jnp.int32, (channels, columns), 1)
+    for k in range(slabs_ref.shape[0]):
+        slab = jnp.broadcast_to(compact_ref[:, pl.ds(k, 1)], (channels, columns))
+        if k < 27 * layers and k % 3 == 0:
+            slab = jnp.where(lane == 0, 0.0, slab)
+        if k < 27 * layers and k % 3 == 2:
+            slab = jnp.where(lane == columns - 1, 0.0, slab)
+        slabs_ref[k] = slab
     tail = 28 * layers
     gain_ref, bias_ref, read_ref = slabs_ref.at[tail], slabs_ref.at[tail + 1], slabs_ref.at[tail + 2]
     groups = channels // 8
@@ -232,12 +240,7 @@
         ],
         axis=0,
     )
-    slabs = jnp.broadcast_to(stacked[..., None], stacked.shape + (columns,))
-    lane = jnp.arange(columns)
-    side = jnp.arange(stacked.shape[0]) % 3
-    tap_rows = jnp.arange(stacked.shape[0]) < 27 * layers
-    cancel = tap_rows[:, None] & (((side[:, None] == 0) & (lane == 0)) | ((side[:, None] == 2) & (lane == columns - 1)))
-    slabs = jnp.where(cancel[:, None, :], 0.0, slabs)
+    compact = jnp.transpose(stacked)
     mix = jnp.transpose(point_weight, (0, 2, 1)).astype(jnp.bfloat16)
     vmem = pl.BlockSpec(memory_space=pltpu.VMEM)
     return pl.pallas_call(
@@ -248,9 +251,10 @@
         scratch_shapes=[
             pltpu.VMEM((2, extended, channels, rounds * columns), jnp.float32),
             pltpu.VMEM((channels, rounds * columns), jnp.float32),
+            pltpu.VMEM((stacked.shape[0], channels, columns), jnp.float32),
         ],
         compiler_params=pltpu.CompilerParams(vmem_limit_bytes=56 * 1024 * 1024),
-    )(planes, slabs, mix)
+    )(planes, compact, mix)
 
 
 def shards(

time: 66.8 us -> 75.7 us (1.13)
  Pallas kernels: 58 us -> 67.8 us
  other arithmetic: 3.53 us -> 0.01 us
  local copies, waits for them, and re-layouts: 4.92 us -> 7.4 us
    pallas_call x1, Pallas kernels: 38.8 us -> 48.6 us  [run_network(): pl.pallas_call(functools.partial(network_kernel, rows, halo, layers), out...]
    select_n x1 -> x0, other arithmetic: 2.72 us -> none  [run_network(): slabs = jnp.where(cancel[:, None, :], 0.0, slabs)]
    unnamed x7 -> x16, local copies, waits for them, and re-layouts: 0.73 us -> 3.38 us
    reshape x1 -> x2, local copies, waits for them, and re-layouts: 0.01 us -> 1.05 us  [run_network(): jnp.transpose(depth_kernel, (0, 2, 1)).reshape(-1, channels)]
    transpose x1 -> x0, local copies, waits for them, and re-layouts: 0.82 us -> none  [run_network(): jnp.transpose(depth_kernel, (0, 2, 1)).reshape(-1, channels)]
where the time goes in v5:
time: 75.7 us; the launch traced here: 75.2 us
  Pallas kernels  67.8 us (90%)
  local copies, waits for them, and re-layouts  7.4 us (10%)
    pallas_call x1, Pallas kernels, run_network(): pl.pallas_call(functools.partial(network_kernel, rows, halo, layers), out...  48.6 us
    pallas_call x1, Pallas kernels, gather_window(): pl.pallas_call(functools.partial(exchange_kernel, axis_names, halo), out_...  19.2 us
    unnamed x16, local copies, waits for them, and re-layouts  3.38 us

profile of v5, /device:TPU:41, one launch (start us, length us, event | category | flops | bytes accessed | tf_op | source)
XLA Modules:
  0.0 75.2 jit_solution(6453822021209691966)
XLA Ops:
  0.0 0.9 %copy.25 = f32[4,27,64]{1,0,2:T(4,128)S(1)} copy(f32[4,27,64]{2,0,1:T(4,128)} %bitcast.20) | data formatting | bytes 55296 | tf_op jit(solution)/shard_map/reshape | solution.py:235
  0.9 0.0 copy-start.6
  0.9 0.1 reshape.9
  1.1 0.5 copy-done.6
  1.6 0.0 copy-start.3
  1.6 0.1 copy.22
  1.7 0.6 copy-done.3
  2.3 0.1 copy.19
  2.4 0.0 copy-start.4
  2.4 0.7 copy-done.4
  3.0 0.1 copy.20
  3.1 0.0 copy-start.5
  3.1 0.7 copy-done.5
  3.8 0.1 copy.21
  3.9 0.0 copy-start
  3.9 0.7 concatenate.3
  4.6 0.1 copy-done
  4.7 0.0 copy-start.1
  4.7 0.0 copy-start.2
  4.7 0.7 copy.23
  5.4 0.0 copy-done.1
  5.4 0.0 copy-done.2
  5.5 0.6 copy.28
  6.1 19.2 %shard_map.82.planes_ref = bf16[8,12,2,128]{3,2,1,0:T(2,128)(2,1)} custom-call(bf16[2,4,2,128]{3,2,1,0:T(2,128)(2,1)} %bitcast.22), custom_call_target="tpu_custom_call" | custom-call | tf_op jit(solution)/shard_map/pallas_call | solution.py:125
  25.3 48.6 %shard_map.83 = f32[4,16,128]{2,1,0:T(8,128)} custom-call(bf16[8,12,2,128]{3,2,1,0:T(2,128)(2,1)} %shard_map.82.planes_ref, f32[64,115]{1,0:T(8,128)} %bitcast.19, bf16[4,64,64]{2,1,0:T(8,128)(2,1)} %bitcast.17), custom_call_target="tpu_custom_call" | custom-call | tf_op jit(solution)/shard_map/pallas_call | solution.py:246
  73.8 1.4 %copy.24 = f32[1,16,4,128]{3,2,1,0:T(4,128)} copy(f32[1,16,4,128]{3,1,2,0:T(8,128)} %bitcast.18) | data formatting | bytes 65536 | tf_op jit(solution)/shard_map/broadcast_in_dim | solution.py:278
  (2 shorter events, 0.0 us)
Async XLA Ops:
  0.9 0.7 copy-start.6
  1.6 0.7 copy-start.3
  2.4 0.7 copy-start.4
  3.1 0.7 copy-start.5
  3.9 0.8 %copy-start = (bf16[4,64,64]{2,1,0:T(8,128)(2,1)S(1)}, bf16[4,64,64]{2,1,0:T(8,128)(2,1)}, u32[]{:S(2)}) copy-start(bf16[4,64,64]{2,1,0:T(8,128)(2,1)} %param.13) | copy-start | bytes 98308
  4.7 0.7 copy-start.1
  4.7 0.7 copy-start.2

commit v6 on v4

--- a/solution.py
+++ b/solution.py
@@ -139,18 +139,32 @@
 
 
 def gelu(value):
-    return 0.5 * value * (1.0 + jnp.tanh(0.7978845608028654 * (value + 0.044715 * (value * value * value))))
-
-
-def network_kernel(rows, halo, layers, planes_ref, slabs_ref, mix_ref, out_ref, feats, depth):
+    half = 0.5 * value
+    inner = value * (0.7978845608028654 + 0.035677408136300125 * (value * value))
+    return half + half * jnp.tanh(inner)
+
+
+def network_kernel(rows, halo, layers, planes_ref, slabs_hbm, mix_ref, out_ref, feats, depth, slabs_ref, slab_sems):
     span, extended, commit, columns = planes_ref.shape
     rounds = span * commit
     channels = slabs_ref.shape[1]
-    tail = 28 * layers
-    gain_ref, bias_ref, read_ref = slabs_ref.at[tail], slabs_ref.at[tail + 1], slabs_ref.at[tail + 2]
+    early = 3 + layers + 27
+    total_slabs = slabs_ref.shape[0]
+    fetch_early = pltpu.make_async_copy(
+        slabs_hbm.at[pl.ds(0, early)], slabs_ref.at[pl.ds(0, early)], slab_sems.at[0]
+    )
+    fetch_late = pltpu.make_async_copy(
+        slabs_hbm.at[pl.ds(early, total_slabs - early)],
+        slabs_ref.at[pl.ds(early, total_slabs - early)],
+        slab_sems.at[1],
+    )
+    fetch_early.start()
+    fetch_late.start()
+    gain_ref, bias_ref, read_ref = slabs_ref.at[0], slabs_ref.at[1], slabs_ref.at[2]
     groups = channels // 8
     tiles = lax.axis_size("tile")
     first_row = lax.axis_index("tile") * rows - halo
+    fetch_early.wait()
 
     def inside(row):
         plane_row = first_row + row
@@ -171,13 +185,15 @@
         return (pltpu.roll(value, 1, 1), value, pltpu.roll(value, columns - 1, 1))
 
     for layer in range(layers):
+        if layer == 1:
+            fetch_late.wait()
         src, dst = layer % 2, (layer + 1) % 2
         last = layer == layers - 1
 
         def one_row(row, carry, layer=layer, src=src, dst=dst, last=last):
             def one_group(group, inner):
                 lanes8 = pl.ds(pl.multiple_of(group * 8, 8), 8)
-                weights = [slabs_ref[27 * layer + tap, lanes8, :] for tap in range(27)]
+                weights = [slabs_ref[3 + layers + 27 * layer + tap, lanes8, :] for tap in range(27)]
                 running = {}
                 for source in range(rounds):
                     cut = pl.ds(source * columns, columns)
@@ -204,7 +220,7 @@
             sums = []
             for t in range(rounds):
                 cut = pl.ds(t * columns, columns)
-                activated = gelu(mixed[:, t * columns : (t + 1) * columns] + slabs_ref[27 * layers + layer])
+                activated = gelu(mixed[:, t * columns : (t + 1) * columns] + slabs_ref[3 + layer])
                 value = (feats[src, row, :, cut] + activated).astype(jnp.bfloat16).astype(jnp.float32)
                 value = jnp.where(keep, value, 0.0)
                 if last:
@@ -224,18 +240,19 @@
     layers, channels, _ = depth_kernel.shape
     stacked = jnp.concatenate(
         [
-            jnp.transpose(depth_kernel, (0, 2, 1)).reshape(-1, channels),
-            point_bias,
             embed_gain[None],
             embed_bias[None],
             read_weight.astype(jnp.float32)[None],
+            point_bias,
+            jnp.transpose(depth_kernel, (0, 2, 1)).reshape(-1, channels),
         ],
         axis=0,
     )
     slabs = jnp.broadcast_to(stacked[..., None], stacked.shape + (columns,))
     lane = jnp.arange(columns)
-    side = jnp.arange(stacked.shape[0]) % 3
-    tap_rows = jnp.arange(stacked.shape[0]) < 27 * layers
+    tap_index = jnp.arange(stacked.shape[0]) - (3 + layers)
+    side = tap_index % 3
+    tap_rows = tap_index >= 0
     cancel = tap_rows[:, None] & (((side[:, None] == 0) & (lane == 0)) | ((side[:, None] == 2) & (lane == columns - 1)))
     slabs = jnp.where(cancel[:, None, :], 0.0, slabs)
     mix = jnp.transpose(point_weight, (0, 2, 1)).astype(jnp.bfloat16)
@@ -243,11 +260,13 @@
     return pl.pallas_call(
         functools.partial(network_kernel, rows, halo, layers),
         out_shape=jax.ShapeDtypeStruct((rows, rounds, columns), jnp.float32),
-        in_specs=[vmem] * 3,
+        in_specs=[vmem, pl.BlockSpec(memory_space=pl.ANY), vmem],
         out_specs=vmem,
         scratch_shapes=[
             pltpu.VMEM((2, extended, channels, rounds * columns), jnp.float32),
             pltpu.VMEM((channels, rounds * columns), jnp.float32),
+            pltpu.VMEM(slabs.shape, jnp.float32),
+            pltpu.SemaphoreType.DMA((2,)),
         ],
         compiler_params=pltpu.CompilerParams(vmem_limit_bytes=56 * 1024 * 1024),
     )(planes, slabs, mix)

time: 66.8 us -> 76.1 us (1.14)
  Pallas kernels: 58 us -> 67.7 us
    pallas_call x1, Pallas kernels: 38.8 us -> 48.4 us  [run_network(): pl.pallas_call(functools.partial(network_kernel, rows, halo, layers), out...]
where the time goes in v6:
time: 76.1 us; the launch traced here: 75.8 us
  Pallas kernels  67.7 us (89%)
  local copies, waits for them, and re-layouts  4.48 us (6%)
  other arithmetic  3.58 us (5%)
    pallas_call x1, Pallas kernels, run_network(): pl.pallas_call(functools.partial(network_kernel, rows, halo, layers), out...  48.4 us
    pallas_call x1, Pallas kernels, gather_window(): pl.pallas_call(functools.partial(exchange_kernel, axis_names, halo), out_...  19.2 us
    select_n x1, other arithmetic, run_network(): slabs = jnp.where(cancel[:, None, :], 0.0, slabs)  2.76 us

profile of v6, /device:TPU:41, one launch (start us, length us, event | category | flops | bytes accessed | tf_op | source)
XLA Modules:
  0.0 75.8 jit_solution(2629409983740214322)
XLA Ops:
  0.0 0.0 copy-start
  0.0 0.0 copy-start.2
  0.0 0.0 copy-start.1
  0.1 0.1 or_and_fusion
  0.2 0.8 %copy.12 = f32[4,27,64]{2,1,0:T(8,128)S(1)} copy(f32[4,27,64]{2,0,1:T(4,128)} %bitcast.16) | data formatting | bytes 55296 | tf_op jit(solution)/shard_map/transpose | solution.py:247
  1.0 0.7 bitcast_convert_fusion
  1.7 0.9 %concatenate.3 = f32[115,64]{1,0:T(8,128)S(1)} concatenate(f32[1,64]{1,0:T(1,128)} %bitcast.19, f32[1,64]{1,0:T(1,128)} %bitcast.20, f32[1,64]{1,0:T(1,128)S(1)} %bitcast_convert_fusion, f32[4,64]{1,0:T(4,128)} %param.14, f32[108,64]{1,0:T(8,128)S(1)} %reshape.94), dimensions={0} | concatenate | bytes 58880 | tf_op jit(solution)/shard_map/concatenate | solution.py:241
  2.6 2.8 %broadcast_select_fusion.slabs_hbm = f32[115,64,128]{2,1,0:T(8,128)} fusion(f32[115,64]{1,0:T(8,128)S(1)} %concatenate.3, pred[115,128]{1,0:T(8,128)(4,1)S(1)} %or_and_fusion), kind=kLoop, calls=%fused_computation | loop fusion | flops 942080 | bytes 3812480 | tf_op jit(solution)/shard_map/jit(_where)/select_n | solution.py:257
  5.4 0.0 copy-done
  5.4 0.7 copy.13
  6.1 0.0 copy-done.2
  6.1 0.0 copy-done.1
  6.1 0.6 copy.16
  6.7 19.2 %shard_map.82.planes_ref = bf16[8,12,2,128]{3,2,1,0:T(2,128)(2,1)} custom-call(bf16[2,4,2,128]{3,2,1,0:T(2,128)(2,1)} %bitcast.18), custom_call_target="tpu_custom_call" | custom-call | tf_op jit(solution)/shard_map/pallas_call | solution.py:125
  26.0 48.4 %shard_map.83 = f32[4,16,128]{2,1,0:T(8,128)} custom-call(bf16[8,12,2,128]{3,2,1,0:T(2,128)(2,1)} %shard_map.82.planes_ref, f32[115,64,128]{2,1,0:T(8,128)} %broadcast_select_fusion.slabs_hbm, bf16[4,64,64]{2,1,0:T(8,128)(2,1)} %bitcast.14), custom_call_target="tpu_custom_call" | custom-call | tf_op jit(solution)/shard_map/pallas_call | solution.py:260
  74.4 1.4 %copy.14 = f32[1,16,4,128]{3,2,1,0:T(4,128)} copy(f32[1,16,4,128]{3,1,2,0:T(8,128)} %bitcast.15) | data formatting | bytes 65536 | tf_op jit(solution)/shard_map/broadcast_in_dim | solution.py:293
  (5 shorter events, 0.1 us)
Async XLA Ops:
  0.0 5.4 %copy-start = (bf16[4,64,64]{2,1,0:T(8,128)(2,1)S(1)}, bf16[4,64,64]{2,1,0:T(8,128)(2,1)}, u32[]{:S(2)}) copy-start(bf16[4,64,64]{2,1,0:T(8,128)(2,1)} %param.13) | copy-start | bytes 98308
  0.0 6.1 %copy-start.2 = (s32[4,4,128]{2,1,0:T(4,128)S(1)}, s32[4,4,128]{2,1,0:T(4,128)}, u32[]{:S(2)}) copy-start(s32[4,4,128]{2,1,0:T(4,128)} %param.8) | copy-start | bytes 24580
  0.0 6.1 %copy-start.1 = (f32[4,4,128]{2,1,0:T(4,128)S(1)}, f32[4,4,128]{2,1,0:T(4,128)}, u32[]{:S(2)}) copy-start(f32[4,4,128]{2,1,0:T(4,128)} %param.9) | copy-start | bytes 24580

commit v7 on v4

--- a/solution.py
+++ b/solution.py
@@ -139,7 +139,9 @@
 
 
 def gelu(value):
-    return 0.5 * value * (1.0 + jnp.tanh(0.7978845608028654 * (value + 0.044715 * (value * value * value))))
+    half = 0.5 * value
+    inner = value * (0.7978845608028654 + 0.035677408136300125 * (value * value))
+    return half + half * jnp.tanh(inner)
 
 
 def network_kernel(rows, halo, layers, planes_ref, slabs_ref, mix_ref, out_ref, feats, depth):

time: 66.8 us -> 66.6 us (level)
  no operation moved by 1% of the time
where the time goes in v7:
time: 66.6 us; the launch traced here: 66.3 us
  Pallas kernels  57.8 us (87%)
  local copies, waits for them, and re-layouts  4.92 us (7%)
  other arithmetic  3.53 us (5%)
    pallas_call x1, Pallas kernels, run_network(): pl.pallas_call(functools.partial(network_kernel, rows, halo, layers), out...  38.5 us
    pallas_call x1, Pallas kernels, gather_window(): pl.pallas_call(functools.partial(exchange_kernel, axis_names, halo), out_...  19.2 us
    select_n x1, other arithmetic, run_network(): slabs = jnp.where(cancel[:, None, :], 0.0, slabs)  2.72 us
    concatenate x1, local copies, waits for them, and re-layouts, run_network(): jnp.concatenate([jnp.transpose(depth_kernel, (0, 2, 1)).reshape(-1, chann...  1.39 us
    broadcast_in_dim x1, local copies, waits for them, and re-layouts, shards(): return jnp.transpose(logits, (1, 0, 2))[None]  1.39 us

profile of v7, /device:TPU:41, one launch (start us, length us, event | category | flops | bytes accessed | tf_op | source)
XLA Modules:
  0.0 66.3 jit_solution(15865968129356228714)
XLA Ops:
  0.0 0.0 copy-start
  0.0 0.0 copy-start.2
  0.0 0.0 copy-start.1
  0.1 0.1 or_and_fusion
  0.2 0.8 %copy.12 = f32[4,27,64]{2,1,0:T(8,128)S(1)} copy(f32[4,27,64]{2,0,1:T(4,128)} %bitcast.16) | data formatting | bytes 55296 | tf_op jit(solution)/shard_map/transpose | solution.py:229
  1.0 0.7 bitcast_convert_fusion
  1.7 1.4 %concatenate.3 = f32[115,64]{1,0:T(8,128)S(1)} concatenate(f32[108,64]{1,0:T(8,128)S(1)} %reshape.94, f32[4,64]{1,0:T(4,128)} %param.14, f32[1,64]{1,0:T(1,128)} %bitcast.19, f32[1,64]{1,0:T(1,128)} %bitcast.20, f32[1,64]{1,0:T(1,128)S(1)} %bitcast_convert_fusion), dimensions={0} | concatenate | bytes 58880 | tf_op jit(solution)/shard_map/concatenate | solution.py:227
  3.1 2.7 %broadcast_select_fusion.slabs_ref = f32[115,64,128]{2,1,0:T(8,128)} fusion(f32[115,64]{1,0:T(8,128)S(1)} %concatenate.3, pred[115,128]{1,0:T(8,128)(4,1)S(1)} %or_and_fusion), kind=kLoop, calls=%fused_computation | loop fusion | flops 942080 | bytes 3812480 | tf_op jit(solution)/shard_map/jit(_where)/select_n | solution.py:242
  5.8 0.0 copy-done
  5.8 0.7 %copy.13 = bf16[4,64,64]{1,2,0:T(8,128)(2,1)} copy(bf16[4,64,64]{2,1,0:T(8,128)(2,1)S(1)} %copy-done) | data formatting | bytes 65536 | tf_op args[5]
  6.5 0.0 copy-done.2
  6.5 0.0 copy-done.1
  6.5 0.6 copy.16
  7.1 19.2 %shard_map.82.planes_ref = bf16[8,12,2,128]{3,2,1,0:T(2,128)(2,1)} custom-call(bf16[2,4,2,128]{3,2,1,0:T(2,128)(2,1)} %bitcast.18), custom_call_target="tpu_custom_call" | custom-call | tf_op jit(solution)/shard_map/pallas_call | solution.py:125
  26.4 38.5 %shard_map.83 = f32[4,16,128]{2,1,0:T(8,128)} custom-call(bf16[8,12,2,128]{3,2,1,0:T(2,128)(2,1)} %shard_map.82.planes_ref, f32[115,64,128]{2,1,0:T(8,128)} %broadcast_select_fusion.slabs_ref, bf16[4,64,64]{2,1,0:T(8,128)(2,1)} %bitcast.14), custom_call_target="tpu_custom_call" | custom-call | tf_op jit(solution)/shard_map/pallas_call | solution.py:245
  64.9 1.4 %copy.14 = f32[1,16,4,128]{3,2,1,0:T(4,128)} copy(f32[1,16,4,128]{3,1,2,0:T(8,128)} %bitcast.15) | data formatting | bytes 65536 | tf_op jit(solution)/shard_map/broadcast_in_dim | solution.py:276
  (5 shorter events, 0.0 us)
Async XLA Ops:
  0.0 5.8 %copy-start = (bf16[4,64,64]{2,1,0:T(8,128)(2,1)S(1)}, bf16[4,64,64]{2,1,0:T(8,128)(2,1)}, u32[]{:S(2)}) copy-start(bf16[4,64,64]{2,1,0:T(8,128)(2,1)} %param.13) | copy-start | bytes 98308
  0.0 6.5 %copy-start.2 = (s32[4,4,128]{2,1,0:T(4,128)S(1)}, s32[4,4,128]{2,1,0:T(4,128)}, u32[]{:S(2)}) copy-start(s32[4,4,128]{2,1,0:T(4,128)} %param.8) | copy-start | bytes 24580
  0.0 6.5 %copy-start.1 = (f32[4,4,128]{2,1,0:T(4,128)S(1)}, f32[4,4,128]{2,1,0:T(4,128)}, u32[]{:S(2)}) copy-start(f32[4,4,128]{2,1,0:T(4,128)} %param.9) | copy-start | bytes 24580

commit v8 on v7

--- a/solution.py
+++ b/solution.py
@@ -214,7 +214,8 @@
                 else:
                     feats[dst, row, :, cut] = value
             if last:
-                out_ref[row - halo] = jnp.concatenate(sums, axis=0)
+                for t in range(rounds):
+                    out_ref[t, pl.ds(row - halo, 1), :] = sums[t]
             return carry
 
         lax.fori_loop(layer + 1, extended - layer - 1, one_row, 0)
@@ -244,7 +245,7 @@
     vmem = pl.BlockSpec(memory_space=pltpu.VMEM)
     return pl.pallas_call(
         functools.partial(network_kernel, rows, halo, layers),
-        out_shape=jax.ShapeDtypeStruct((rows, rounds, columns), jnp.float32),
+        out_shape=jax.ShapeDtypeStruct((rounds, rows, columns), jnp.float32),
         in_specs=[vmem] * 3,
         out_specs=vmem,
         scratch_shapes=[
@@ -273,7 +274,7 @@
     logits = run_network(
         planes, embed_gain, embed_bias, depth_kernel, point_weight, point_bias, read_weight, rows, layers
     )
-    return jnp.transpose(logits, (1, 0, 2))[None]
+    return logits[None]
 
 
 def solution(mesh):

time: 66.6 us -> 65.1 us (0.977)
  local copies, waits for them, and re-layouts: 4.92 us -> 3.54 us
    broadcast_in_dim x1 -> x0, local copies, waits for them, and re-layouts: 1.39 us -> none  [shards(): return jnp.transpose(logits, (1, 0, 2))[None]]
where the time goes in v8:
time: 65.1 us; the launch traced here: 64.9 us
  Pallas kernels  57.8 us (89%)
  local copies, waits for them, and re-layouts  3.54 us (5%)
  other arithmetic  3.53 us (5%)
    pallas_call x1, Pallas kernels, run_network(): pl.pallas_call(functools.partial(network_kernel, rows, halo, layers), out...  38.6 us
    pallas_call x1, Pallas kernels, gather_window(): pl.pallas_call(functools.partial(exchange_kernel, axis_names, halo), out_...  19.2 us
    select_n x1, other arithmetic, run_network(): slabs = jnp.where(cancel[:, None, :], 0.0, slabs)  2.72 us
    concatenate x1, local copies, waits for them, and re-layouts, run_network(): jnp.concatenate([jnp.transpose(depth_kernel, (0, 2, 1)).reshape(-1, chann...  1.39 us

profile of v8, /device:TPU:41, one launch (start us, length us, event | category | flops | bytes accessed | tf_op | source)
XLA Modules:
  0.0 64.9 jit_solution(1883088754421911862)
XLA Ops:
  0.0 0.0 copy-start
  0.0 0.0 copy-start.2
  0.0 0.0 copy-start.1
  0.1 0.1 or_and_fusion
  0.2 0.8 %copy.11 = f32[4,27,64]{2,1,0:T(8,128)S(1)} copy(f32[4,27,64]{2,0,1:T(4,128)} %bitcast.13) | data formatting | bytes 55296 | tf_op jit(solution)/shard_map/transpose | solution.py:230
  1.0 0.7 %bitcast_convert_fusion = f32[1,64]{1,0:T(1,128)S(1)} fusion(bf16[64]{0:T(256)(128)(2,1)} %param.15), kind=kLoop, calls=%fused_computation.5 | loop fusion | flops 64 | bytes 384 | tf_op jit(solution)/shard_map/broadcast_in_dim | solution.py:234
  1.7 1.4 %concatenate.3 = f32[115,64]{1,0:T(8,128)S(1)} concatenate(f32[108,64]{1,0:T(8,128)S(1)} %reshape.94, f32[4,64]{1,0:T(4,128)} %param.14, f32[1,64]{1,0:T(1,128)} %bitcast.16, f32[1,64]{1,0:T(1,128)} %bitcast.17, f32[1,64]{1,0:T(1,128)S(1)} %bitcast_convert_fusion), dimensions={0} | concatenate | bytes 58880 | tf_op jit(solution)/shard_map/concatenate | solution.py:228
  3.1 2.7 %broadcast_select_fusion.slabs_ref = f32[115,64,128]{2,1,0:T(8,128)} fusion(f32[115,64]{1,0:T(8,128)S(1)} %concatenate.3, pred[115,128]{1,0:T(8,128)(4,1)S(1)} %or_and_fusion), kind=kLoop, calls=%fused_computation | loop fusion | flops 942080 | bytes 3812480 | tf_op jit(solution)/shard_map/jit(_where)/select_n | solution.py:243
  5.8 0.0 copy-done
  5.8 0.7 %copy.12 = bf16[4,64,64]{1,2,0:T(8,128)(2,1)} copy(bf16[4,64,64]{2,1,0:T(8,128)(2,1)S(1)} %copy-done) | data formatting | bytes 65536 | tf_op args[5]
  6.5 0.0 copy-done.2
  6.5 0.0 copy-done.1
  6.5 0.6 copy.14
  7.1 19.2 %shard_map.82.planes_ref = bf16[8,12,2,128]{3,2,1,0:T(2,128)(2,1)} custom-call(bf16[2,4,2,128]{3,2,1,0:T(2,128)(2,1)} %bitcast.15), custom_call_target="tpu_custom_call" | custom-call | tf_op jit(solution)/shard_map/pallas_call | solution.py:125
  26.4 38.6 %shard_map.83 = f32[16,4,128]{2,1,0:T(4,128)} custom-call(bf16[8,12,2,128]{3,2,1,0:T(2,128)(2,1)} %shard_map.82.planes_ref, f32[115,64,128]{2,1,0:T(8,128)} %broadcast_select_fusion.slabs_ref, bf16[4,64,64]{2,1,0:T(8,128)(2,1)} %bitcast.12), custom_call_target="tpu_custom_call" | custom-call | tf_op jit(solution)/shard_map/pallas_call | solution.py:246
  (5 shorter events, 0.0 us)
Async XLA Ops:
  0.0 5.8 %copy-start = (bf16[4,64,64]{2,1,0:T(8,128)(2,1)S(1)}, bf16[4,64,64]{2,1,0:T(8,128)(2,1)}, u32[]{:S(2)}) copy-start(bf16[4,64,64]{2,1,0:T(8,128)(2,1)} %param.13) | copy-start | bytes 98308
  0.0 6.5 %copy-start.2 = (s32[4,4,128]{2,1,0:T(4,128)S(1)}, s32[4,4,128]{2,1,0:T(4,128)}, u32[]{:S(2)}) copy-start(s32[4,4,128]{2,1,0:T(4,128)} %param.8) | copy-start | bytes 24580
  0.0 6.5 %copy-start.1 = (f32[4,4,128]{2,1,0:T(4,128)S(1)}, f32[4,4,128]{2,1,0:T(4,128)}, u32[]{:S(2)}) copy-start(f32[4,4,128]{2,1,0:T(4,128)} %param.9) | copy-start | bytes 24580

commit v9 on v8

--- a/solution.py
+++ b/solution.py
@@ -199,8 +199,11 @@
                 return inner
 
             lax.fori_loop(0, groups, one_group, 0, unroll=8)
-            mixed = jnp.dot(
-                mix_ref[layer], depth[...].astype(jnp.bfloat16), preferred_element_type=jnp.float32
+            mixed = lax.dot_general(
+                mix_ref[layer],
+                depth[...].astype(jnp.bfloat16),
+                (((0,), (0,)), ((), ())),
+                preferred_element_type=jnp.float32,
             )
             keep = inside(row)
             sums = []
@@ -241,7 +244,7 @@
     tap_rows = jnp.arange(stacked.shape[0]) < 27 * layers
     cancel = tap_rows[:, None] & (((side[:, None] == 0) & (lane == 0)) | ((side[:, None] == 2) & (lane == columns - 1)))
     slabs = jnp.where(cancel[:, None, :], 0.0, slabs)
-    mix = jnp.transpose(point_weight, (0, 2, 1)).astype(jnp.bfloat16)
+    mix = point_weight.astype(jnp.bfloat16)
     vmem = pl.BlockSpec(memory_space=pltpu.VMEM)
     return pl.pallas_call(
         functools.partial(network_kernel, rows, halo, layers),

time: 65.1 us -> 66 us (1.014)
  Pallas kernels: 57.8 us -> 59.4 us
  local copies, waits for them, and re-layouts: 3.54 us -> 2.82 us
    pallas_call x1, Pallas kernels: 38.6 us -> 40.1 us  [run_network(): pl.pallas_call(functools.partial(network_kernel, rows, halo, layers), out...]
    unnamed x7 -> x4, local copies, waits for them, and re-layouts: 0.73 us -> 0.01 us
where the time goes in v9:
time: 66 us; the launch traced here: 65.7 us
  Pallas kernels  59.4 us (90%)
  other arithmetic  3.52 us (5%)
  local copies, waits for them, and re-layouts  2.82 us (4%)
    pallas_call x1, Pallas kernels, run_network(): pl.pallas_call(functools.partial(network_kernel, rows, halo, layers), out...  40.1 us
    pallas_call x1, Pallas kernels, gather_window(): pl.pallas_call(functools.partial(exchange_kernel, axis_names, halo), out_...  19.2 us
    select_n x1, other arithmetic, run_network(): slabs = jnp.where(cancel[:, None, :], 0.0, slabs)  2.7 us
    concatenate x1, local copies, waits for them, and re-layouts, run_network(): jnp.concatenate([jnp.transpose(depth_kernel, (0, 2, 1)).reshape(-1, chann...  1.39 us

profile of v9, /device:TPU:41, one launch (start us, length us, event | category | flops | bytes accessed | tf_op | source)
XLA Modules:
  0.0 65.7 jit_solution(15618481526874172377)
XLA Ops:
  0.0 0.0 copy-start.1
  0.0 0.0 copy-start
  0.0 0.1 or_and_fusion
  0.2 0.8 %copy.10 = f32[4,27,64]{2,1,0:T(8,128)S(1)} copy(f32[4,27,64]{2,0,1:T(4,128)} %bitcast.11) | data formatting | bytes 55296 | tf_op jit(solution)/shard_map/transpose | solution.py:233
  1.0 0.7 %bitcast_convert_fusion = f32[1,64]{1,0:T(1,128)S(1)} fusion(bf16[64]{0:T(256)(128)(2,1)} %param.15), kind=kLoop, calls=%fused_computation.5 | loop fusion | flops 64 | bytes 384 | tf_op jit(solution)/shard_map/broadcast_in_dim | solution.py:237
  1.7 1.4 %concatenate.3 = f32[115,64]{1,0:T(8,128)S(1)} concatenate(f32[108,64]{1,0:T(8,128)S(1)} %reshape.94, f32[4,64]{1,0:T(4,128)} %param.14, f32[1,64]{1,0:T(1,128)} %bitcast.14, f32[1,64]{1,0:T(1,128)} %bitcast.15, f32[1,64]{1,0:T(1,128)S(1)} %bitcast_convert_fusion), dimensions={0} | concatenate | bytes 58880 | tf_op jit(solution)/shard_map/concatenate | solution.py:231
  3.0 2.7 %broadcast_select_fusion.slabs_ref = f32[115,64,128]{2,1,0:T(8,128)} fusion(f32[115,64]{1,0:T(8,128)S(1)} %concatenate.3, pred[115,128]{1,0:T(8,128)(4,1)S(1)} %or_and_fusion), kind=kLoop, calls=%fused_computation | loop fusion | flops 942080 | bytes 3812480 | tf_op jit(solution)/shard_map/jit(_where)/select_n | solution.py:246
  5.7 0.0 copy-done.1
  5.8 0.0 copy-done
  5.8 0.6 copy.12
  6.4 19.2 %shard_map.82.planes_ref = bf16[8,12,2,128]{3,2,1,0:T(2,128)(2,1)} custom-call(bf16[2,4,2,128]{3,2,1,0:T(2,128)(2,1)} %bitcast.13), custom_call_target="tpu_custom_call" | custom-call | tf_op jit(solution)/shard_map/pallas_call | solution.py:125
  25.6 40.1 %shard_map.83 = f32[16,4,128]{2,1,0:T(4,128)} custom-call(bf16[8,12,2,128]{3,2,1,0:T(2,128)(2,1)} %shard_map.82.planes_ref, f32[115,64,128]{2,1,0:T(8,128)} %broadcast_select_fusion.slabs_ref, bf16[4,64,64]{2,1,0:T(8,128)(2,1)} %mix_ref.1), custom_call_target="tpu_custom_call" | custom-call | tf_op jit(solution)/shard_map/pallas_call | solution.py:249
  (5 shorter events, 0.0 us)
Async XLA Ops:
  0.0 5.8 %copy-start.1 = (s32[4,4,128]{2,1,0:T(4,128)S(1)}, s32[4,4,128]{2,1,0:T(4,128)}, u32[]{:S(2)}) copy-start(s32[4,4,128]{2,1,0:T(4,128)} %param.8) | copy-start | bytes 24580
  0.0 5.8 %copy-start = (f32[4,4,128]{2,1,0:T(4,128)S(1)}, f32[4,4,128]{2,1,0:T(4,128)}, u32[]{:S(2)}) copy-start(f32[4,4,128]{2,1,0:T(4,128)} %param.9) | copy-start | bytes 24580

commit v10 on v8

--- a/solution.py
+++ b/solution.py
@@ -33,11 +33,18 @@
         held[:, pl.ds(rows + halo, halo)] = blank
 
     neighbour_tiles = 1 + (tile > 0).astype(jnp.int32) + (tile < tiles - 1).astype(jnp.int32)
+
+    def linked(other):
+        sends = (other >= win * pieces - span + 1) & (other <= win * pieces + pieces - 1)
+        takes = (other * pieces <= win + span - 1) & ((other + 1) * pieces - 1 >= win)
+        return sends | takes
+
+    linked_wins = sum(linked(other).astype(jnp.int32) for other in range(wins))
     barrier = pltpu.get_barrier_semaphore()
     for shift in (-1, 0, 1):
         for other in range(wins):
             there = tile + shift
-            partner = (there >= 0) & (there < tiles)
+            partner = (there >= 0) & (there < tiles) & linked(other)
             if shift == 0:
                 partner = partner & (win != other)
 
@@ -45,7 +52,7 @@
             def _():
                 pl.semaphore_signal(barrier, 1, device_id=device(there, other), device_id_type=mesh_ids)
 
-    pl.semaphore_wait(barrier, neighbour_tiles * wins - 1)
+    pl.semaphore_wait(barrier, neighbour_tiles * linked_wins - 1)
 
     parts = ((-1, 0, rows + halo, halo, 0), (0, 0, halo, rows, 1), (1, rows - halo, 0, halo, 0))
     started = []

time: 65.1 us -> 65 us (level)
  the two profiles are of different devices: /device:TPU:41 before, /device:TPU:49 now
where the time goes in v10:
time: 65 us; the launch traced here: 64.8 us
  Pallas kernels  57.6 us (89%)
  local copies, waits for them, and re-layouts  3.54 us (5%)
  other arithmetic  3.53 us (5%)
    pallas_call x1, Pallas kernels, run_network(): pl.pallas_call(functools.partial(network_kernel, rows, halo, layers), out...  38.6 us
    pallas_call x1, Pallas kernels, gather_window(): pl.pallas_call(functools.partial(exchange_kernel, axis_names, halo), out_...  19.1 us
    select_n x1, other arithmetic, run_network(): slabs = jnp.where(cancel[:, None, :], 0.0, slabs)  2.72 us
    concatenate x1, local copies, waits for them, and re-layouts, run_network(): jnp.concatenate([jnp.transpose(depth_kernel, (0, 2, 1)).reshape(-1, chann...  1.39 us

profile of v10, /device:TPU:49, one launch (start us, length us, event | category | flops | bytes accessed | tf_op | source)
XLA Modules:
  0.0 64.8 jit_solution(17982898467114804808)
XLA Ops:
  0.0 0.0 copy-start
  0.0 0.0 copy-start.2
  0.0 0.0 copy-start.1
  0.1 0.1 or_and_fusion
  0.2 0.8 %copy.11 = f32[4,27,64]{2,1,0:T(8,128)S(1)} copy(f32[4,27,64]{2,0,1:T(4,128)} %bitcast.13) | data formatting | bytes 55296 | tf_op jit(solution)/shard_map/transpose | solution.py:237
  1.0 0.7 %bitcast_convert_fusion = f32[1,64]{1,0:T(1,128)S(1)} fusion(bf16[64]{0:T(256)(128)(2,1)} %param.15), kind=kLoop, calls=%fused_computation.5 | loop fusion | flops 64 | bytes 384 | tf_op jit(solution)/shard_map/broadcast_in_dim | solution.py:241
  1.7 1.4 %concatenate.3 = f32[115,64]{1,0:T(8,128)S(1)} concatenate(f32[108,64]{1,0:T(8,128)S(1)} %reshape.94, f32[4,64]{1,0:T(4,128)} %param.14, f32[1,64]{1,0:T(1,128)} %bitcast.16, f32[1,64]{1,0:T(1,128)} %bitcast.17, f32[1,64]{1,0:T(1,128)S(1)} %bitcast_convert_fusion), dimensions={0} | concatenate | bytes 58880 | tf_op jit(solution)/shard_map/concatenate | solution.py:235
  3.1 2.7 %broadcast_select_fusion.slabs_ref = f32[115,64,128]{2,1,0:T(8,128)} fusion(f32[115,64]{1,0:T(8,128)S(1)} %concatenate.3, pred[115,128]{1,0:T(8,128)(4,1)S(1)} %or_and_fusion), kind=kLoop, calls=%fused_computation | loop fusion | flops 942080 | bytes 3812480 | tf_op jit(solution)/shard_map/jit(_where)/select_n | solution.py:250
  5.8 0.0 copy-done
  5.8 0.7 %copy.12 = bf16[4,64,64]{1,2,0:T(8,128)(2,1)} copy(bf16[4,64,64]{2,1,0:T(8,128)(2,1)S(1)} %copy-done) | data formatting | bytes 65536 | tf_op args[5]
  6.5 0.0 copy-done.2
  6.5 0.0 copy-done.1
  6.5 0.6 copy.14
  7.1 19.1 %shard_map.82.planes_ref = bf16[8,12,2,128]{3,2,1,0:T(2,128)(2,1)} custom-call(bf16[2,4,2,128]{3,2,1,0:T(2,128)(2,1)} %bitcast.15), custom_call_target="tpu_custom_call" | custom-call | tf_op jit(solution)/shard_map/pallas_call | solution.py:132
  26.2 38.6 %shard_map.83 = f32[16,4,128]{2,1,0:T(4,128)} custom-call(bf16[8,12,2,128]{3,2,1,0:T(2,128)(2,1)} %shard_map.82.planes_ref, f32[115,64,128]{2,1,0:T(8,128)} %broadcast_select_fusion.slabs_ref, bf16[4,64,64]{2,1,0:T(8,128)(2,1)} %bitcast.12), custom_call_target="tpu_custom_call" | custom-call | tf_op jit(solution)/shard_map/pallas_call | solution.py:253
  (5 shorter events, 0.0 us)
Async XLA Ops:
  0.0 5.8 %copy-start = (bf16[4,64,64]{2,1,0:T(8,128)(2,1)S(1)}, bf16[4,64,64]{2,1,0:T(8,128)(2,1)}, u32[]{:S(2)}) copy-start(bf16[4,64,64]{2,1,0:T(8,128)(2,1)} %param.13) | copy-start | bytes 98308
  0.0 6.5 %copy-start.2 = (s32[4,4,128]{2,1,0:T(4,128)S(1)}, s32[4,4,128]{2,1,0:T(4,128)}, u32[]{:S(2)}) copy-start(s32[4,4,128]{2,1,0:T(4,128)} %param.8) | copy-start | bytes 24580
  0.0 6.5 %copy-start.1 = (f32[4,4,128]{2,1,0:T(4,128)S(1)}, f32[4,4,128]{2,1,0:T(4,128)}, u32[]{:S(2)}) copy-start(f32[4,4,128]{2,1,0:T(4,128)} %param.9) | copy-start | bytes 24580

commit v11 on v8

--- a/solution.py
+++ b/solution.py
@@ -144,12 +144,11 @@
     return half + half * jnp.tanh(inner)
 
 
-def network_kernel(rows, halo, layers, planes_ref, slabs_ref, mix_ref, out_ref, feats, depth):
+def network_kernel(rows, halo, layers, planes_ref, slabs_ref, small_ref, mix_ref, out_ref, feats, depth):
     span, extended, commit, columns = planes_ref.shape
     rounds = span * commit
     channels = slabs_ref.shape[1]
-    tail = 28 * layers
-    gain_ref, bias_ref, read_ref = slabs_ref.at[tail], slabs_ref.at[tail + 1], slabs_ref.at[tail + 2]
+    gain_ref, bias_ref, read_ref = small_ref.at[0], small_ref.at[1], small_ref.at[2]
     groups = channels // 8
     tiles = lax.axis_size("tile")
     first_row = lax.axis_index("tile") * rows - halo
@@ -206,7 +205,7 @@
             sums = []
             for t in range(rounds):
                 cut = pl.ds(t * columns, columns)
-                activated = gelu(mixed[:, t * columns : (t + 1) * columns] + slabs_ref[27 * layers + layer])
+                activated = gelu(mixed[:, t * columns : (t + 1) * columns] + small_ref[3 + layer])
                 value = (feats[src, row, :, cut] + activated).astype(jnp.bfloat16).astype(jnp.float32)
                 value = jnp.where(keep, value, 0.0)
                 if last:
@@ -225,35 +224,28 @@
     span, extended, commit, columns = planes.shape
     rounds = span * commit
     layers, channels, _ = depth_kernel.shape
+    lane = jnp.arange(columns)
+    side = jnp.arange(27) % 3
+    cancel = ((side[:, None] == 0) & (lane == 0)) | ((side[:, None] == 2) & (lane == columns - 1))
+    taps = jnp.broadcast_to(jnp.transpose(depth_kernel, (0, 2, 1))[..., None], (layers, 27, channels, columns))
+    slabs = jnp.where(cancel[None, :, None, :], 0.0, taps).reshape(layers * 27, channels, columns)
     stacked = jnp.concatenate(
-        [
-            jnp.transpose(depth_kernel, (0, 2, 1)).reshape(-1, channels),
-            point_bias,
-            embed_gain[None],
-            embed_bias[None],
-            read_weight.astype(jnp.float32)[None],
-        ],
-        axis=0,
+        [embed_gain[None], embed_bias[None], read_weight.astype(jnp.float32)[None], point_bias], axis=0
     )
-    slabs = jnp.broadcast_to(stacked[..., None], stacked.shape + (columns,))
-    lane = jnp.arange(columns)
-    side = jnp.arange(stacked.shape[0]) % 3
-    tap_rows = jnp.arange(stacked.shape[0]) < 27 * layers
-    cancel = tap_rows[:, None] & (((side[:, None] == 0) & (lane == 0)) | ((side[:, None] == 2) & (lane == columns - 1)))
-    slabs = jnp.where(cancel[:, None, :], 0.0, slabs)
+    small = jnp.broadcast_to(stacked[..., None], stacked.shape + (columns,))
     mix = jnp.transpose(point_weight, (0, 2, 1)).astype(jnp.bfloat16)
     vmem = pl.BlockSpec(memory_space=pltpu.VMEM)
     return pl.pallas_call(
         functools.partial(network_kernel, rows, halo, layers),
         out_shape=jax.ShapeDtypeStruct((rounds, rows, columns), jnp.float32),
-        in_specs=[vmem] * 3,
+        in_specs=[vmem] * 4,
         out_specs=vmem,
         scratch_shapes=[
             pltpu.VMEM((2, extended, channels, rounds * columns), jnp.float32),
             pltpu.VMEM((channels, rounds * columns), jnp.float32),
         ],
         compiler_params=pltpu.CompilerParams(vmem_limit_bytes=56 * 1024 * 1024),
-    )(planes, slabs, mix)
+    )(planes, slabs, small, mix)
 
 
 def shards(

time: 65.1 us -> 63.7 us (0.978)
  other arithmetic: 3.53 us -> 2.71 us
    concatenate x1 -> x0, local copies, waits for them, and re-layouts: 1.39 us -> none  [run_network(): jnp.concatenate([jnp.transpose(depth_kernel, (0, 2, 1)).reshape(-1, chann...]
    broadcast_in_dim x0 -> x4, local copies, waits for them, and re-layouts: none -> 0.84 us  [the longest x1 0.81 us: run_network(): small = jnp.broadcast_to(stacked[..., None], stacked.shape + (columns,))]
    broadcast_in_dim x1, other arithmetic: 0.66 us -> 0.01 us  [run_network(): read_weight.astype(jnp.float32)[None]]
where the time goes in v11:
time: 63.7 us; the launch traced here: 63.6 us
  Pallas kernels  57.7 us (91%)
  local copies, waits for them, and re-layouts  3.01 us (5%)
  other arithmetic  2.71 us (4%)
    pallas_call x1, Pallas kernels, run_network(): pl.pallas_call(functools.partial(network_kernel, rows, halo, layers), out...  38.5 us
    pallas_call x1, Pallas kernels, gather_window(): pl.pallas_call(functools.partial(exchange_kernel, axis_names, halo), out_...  19.2 us
    select_n x1, other arithmetic, run_network(): jnp.where(cancel[None, :, None, :], 0.0, taps)  2.59 us

profile of v11, /device:TPU:41, one launch (start us, length us, event | category | flops | bytes accessed | tf_op | source)
XLA Modules:
  0.0 63.6 jit_solution(15031924535174387968)
XLA Ops:
  0.0 0.0 copy-start.6
  0.0 0.0 copy-start.5
  0.0 0.0 copy-start.4
  0.0 0.0 copy-start.3
  0.0 0.0 copy-start
  0.0 0.0 copy-start.2
  0.0 0.0 copy-start.1
  0.1 0.1 and_or_fusion
  0.2 0.8 %copy.11 = f32[4,27,64]{2,1,0:T(8,128)S(1)} copy(f32[4,27,64]{2,0,1:T(4,128)} %bitcast.13) | data formatting | bytes 55296 | tf_op jit(solution)/shard_map/transpose | solution.py:230
  1.0 2.6 %broadcast_select_fusion.slabs_ref = f32[108,64,128]{2,1,0:T(8,128)} fusion(f32[108,64]{1,0:T(8,128)S(1)} %broadcast_in_dim.54, pred[108,128]{1,0:T(8,128)(4,1)S(1)} %broadcast_in_dim.51), kind=kLoop, calls=%fused_computation | loop fusion | flops 884736 | bytes 3580416 | tf_op jit(solution)/shard_map/jit(_where)/select_n | solution.py:231
  3.6 0.0 copy-done.6
  3.6 0.0 copy-done.5
  3.6 0.0 copy-done.4
  3.6 0.0 copy-done.3
  3.7 0.8 %broadcast_in_dim.60.small_ref = f32[7,64,128]{2,1,0:T(8,128)} broadcast(f32[7,64]{1,0:T(8,128)S(1)} %pad_maximum_fusion), dimensions={0,1} | broadcast | bytes 231168 | tf_op jit(solution)/shard_map/broadcast_in_dim | solution.py:235
  4.5 0.0 copy-done
  4.5 0.7 %copy.12 = bf16[4,64,64]{1,2,0:T(8,128)(2,1)} copy(bf16[4,64,64]{2,1,0:T(8,128)(2,1)S(1)} %copy-done) | data formatting | bytes 65536 | tf_op args[5]
  5.2 0.0 copy-done.2
  5.2 0.0 copy-done.1
  5.2 0.6 copy.14
  5.8 19.2 %shard_map.82.planes_ref = bf16[8,12,2,128]{3,2,1,0:T(2,128)(2,1)} custom-call(bf16[2,4,2,128]{3,2,1,0:T(2,128)(2,1)} %bitcast.15), custom_call_target="tpu_custom_call" | custom-call | tf_op jit(solution)/shard_map/pallas_call | solution.py:125
  25.1 38.5 %shard_map.83 = f32[16,4,128]{2,1,0:T(4,128)} custom-call(bf16[8,12,2,128]{3,2,1,0:T(2,128)(2,1)} %shard_map.82.planes_ref, f32[108,64,128]{2,1,0:T(8,128)} %broadcast_select_fusion.slabs_ref, f32[7,64,128]{2,1,0:T(8,128)} %broadcast_in_dim.60.small_ref, bf16[4,64,64]{2,1,0:T(8,128)(2,1)} %bitcast.12), custom_call_target="tpu_custom_call" | custom-call | tf_op jit(solution)/shard_map/pallas_call | solution.py:238
  (8 shorter events, 0.1 us)
Async XLA Ops:
  0.0 3.6 %copy-start.6 = (bf16[64]{0:T(256)(128)(2,1)S(1)}, bf16[64]{0:T(256)(128)(2,1)}, u32[]{:S(2)}) copy-start(bf16[64]{0:T(256)(128)(2,1)} %param.15) | copy-start | bytes 388
  0.0 3.6 %copy-start.5 = (f32[64]{0:T(128)S(1)}, f32[64]{0:T(128)}, u32[]{:S(2)}) copy-start(f32[64]{0:T(128)} %param.10) | copy-start | bytes 772
  0.0 3.6 %copy-start.4 = (f32[64]{0:T(128)S(1)}, f32[64]{0:T(128)}, u32[]{:S(2)}) copy-start(f32[64]{0:T(128)} %param.11) | copy-start | bytes 772
  0.0 3.6 %copy-start.3 = (f32[4,64]{1,0:T(4,128)S(1)}, f32[4,64]{1,0:T(4,128)}, u32[]{:S(2)}) copy-start(f32[4,64]{1,0:T(4,128)} %param.14) | copy-start | bytes 3076
  0.0 4.5 %copy-start = (bf16[4,64,64]{2,1,0:T(8,128)(2,1)S(1)}, bf16[4,64,64]{2,1,0:T(8,128)(2,1)}, u32[]{:S(2)}) copy-start(bf16[4,64,64]{2,1,0:T(8,128)(2,1)} %param.13) | copy-start | bytes 98308
  0.0 5.2 %copy-start.2 = (s32[4,4,128]{2,1,0:T(4,128)S(1)}, s32[4,4,128]{2,1,0:T(4,128)}, u32[]{:S(2)}) copy-start(s32[4,4,128]{2,1,0:T(4,128)} %param.8) | copy-start | bytes 24580
  0.0 5.2 %copy-start.1 = (f32[4,4,128]{2,1,0:T(4,128)S(1)}, f32[4,4,128]{2,1,0:T(4,128)}, u32[]{:S(2)}) copy-start(f32[4,4,128]{2,1,0:T(4,128)} %param.9) | copy-start | bytes 24580

commit v12 on v11

--- a/solution.py
+++ b/solution.py
@@ -207,11 +207,17 @@
                 cut = pl.ds(t * columns, columns)
                 activated = gelu(mixed[:, t * columns : (t + 1) * columns] + small_ref[3 + layer])
                 value = (feats[src, row, :, cut] + activated).astype(jnp.bfloat16).astype(jnp.float32)
-                value = jnp.where(keep, value, 0.0)
                 if last:
+                    value = jnp.where(keep, value, 0.0)
                     sums.append(jnp.sum(value * read_ref[...], axis=0, keepdims=True))
                 else:
                     feats[dst, row, :, cut] = value
+            if not last:
+
+                @pl.when(jnp.logical_not(keep))
+                def _():
+                    feats[dst, row] = jnp.zeros(feats.shape[2:], jnp.float32)
+
             if last:
                 for t in range(rounds):
                     out_ref[t, pl.ds(row - halo, 1), :] = sums[t]

time: 63.7 us -> 63.2 us (level)
  no operation moved by 1% of the time
where the time goes in v12:
time: 63.2 us; the launch traced here: 63 us
  Pallas kernels  57.2 us (91%)
  local copies, waits for them, and re-layouts  3.01 us (5%)
  other arithmetic  2.71 us (4%)
    pallas_call x1, Pallas kernels, run_network(): pl.pallas_call(functools.partial(network_kernel, rows, halo, layers), out...  37.9 us
    pallas_call x1, Pallas kernels, gather_window(): pl.pallas_call(functools.partial(exchange_kernel, axis_names, halo), out_...  19.2 us
    select_n x1, other arithmetic, run_network(): jnp.where(cancel[None, :, None, :], 0.0, taps)  2.59 us

profile of v12, /device:TPU:41, one launch (start us, length us, event | category | flops | bytes accessed | tf_op | source)
XLA Modules:
  0.0 63.0 jit_solution(8626282119658197489)
XLA Ops:
  0.0 0.0 copy-start.6
  0.0 0.0 copy-start.5
  0.0 0.0 copy-start.4
  0.0 0.0 copy-start.3
  0.0 0.0 copy-start
  0.0 0.0 copy-start.2
  0.0 0.0 copy-start.1
  0.1 0.1 and_or_fusion
  0.2 0.8 %copy.11 = f32[4,27,64]{2,1,0:T(8,128)S(1)} copy(f32[4,27,64]{2,0,1:T(4,128)} %bitcast.13) | data formatting | bytes 55296 | tf_op jit(solution)/shard_map/transpose | solution.py:236
  1.0 2.6 %broadcast_select_fusion.slabs_ref = f32[108,64,128]{2,1,0:T(8,128)} fusion(f32[108,64]{1,0:T(8,128)S(1)} %broadcast_in_dim.54, pred[108,128]{1,0:T(8,128)(4,1)S(1)} %broadcast_in_dim.51), kind=kLoop, calls=%fused_computation | loop fusion | flops 884736 | bytes 3580416 | tf_op jit(solution)/shard_map/jit(_where)/select_n | solution.py:237
  3.6 0.0 copy-done.6
  3.6 0.0 copy-done.5
  3.6 0.0 copy-done.4
  3.6 0.0 copy-done.3
  3.7 0.8 %broadcast_in_dim.60.small_ref = f32[7,64,128]{2,1,0:T(8,128)} broadcast(f32[7,64]{1,0:T(8,128)S(1)} %pad_maximum_fusion), dimensions={0,1} | broadcast | bytes 231168 | tf_op jit(solution)/shard_map/broadcast_in_dim | solution.py:241
  4.5 0.0 copy-done
  4.5 0.7 %copy.12 = bf16[4,64,64]{1,2,0:T(8,128)(2,1)} copy(bf16[4,64,64]{2,1,0:T(8,128)(2,1)S(1)} %copy-done) | data formatting | bytes 65536 | tf_op args[5]
  5.2 0.0 copy-done.2
  5.2 0.0 copy-done.1
  5.2 0.6 copy.14
  5.8 19.2 %shard_map.82.planes_ref = bf16[8,12,2,128]{3,2,1,0:T(2,128)(2,1)} custom-call(bf16[2,4,2,128]{3,2,1,0:T(2,128)(2,1)} %bitcast.15), custom_call_target="tpu_custom_call" | custom-call | tf_op jit(solution)/shard_map/pallas_call | solution.py:125
  25.1 37.9 %shard_map.83 = f32[16,4,128]{2,1,0:T(4,128)} custom-call(bf16[8,12,2,128]{3,2,1,0:T(2,128)(2,1)} %shard_map.82.planes_ref, f32[108,64,128]{2,1,0:T(8,128)} %broadcast_select_fusion.slabs_ref, f32[7,64,128]{2,1,0:T(8,128)} %broadcast_in_dim.60.small_ref, bf16[4,64,64]{2,1,0:T(8,128)(2,1)} %bitcast.12), custom_call_target="tpu_custom_call" | custom-call | tf_op jit(solution)/shard_map/pallas_call | solution.py:244
  (8 shorter events, 0.1 us)
Async XLA Ops:
  0.0 3.6 %copy-start.6 = (bf16[64]{0:T(256)(128)(2,1)S(1)}, bf16[64]{0:T(256)(128)(2,1)}, u32[]{:S(2)}) copy-start(bf16[64]{0:T(256)(128)(2,1)} %param.15) | copy-start | bytes 388
  0.0 3.6 %copy-start.5 = (f32[64]{0:T(128)S(1)}, f32[64]{0:T(128)}, u32[]{:S(2)}) copy-start(f32[64]{0:T(128)} %param.10) | copy-start | bytes 772
  0.0 3.6 %copy-start.4 = (f32[64]{0:T(128)S(1)}, f32[64]{0:T(128)}, u32[]{:S(2)}) copy-start(f32[64]{0:T(128)} %param.11) | copy-start | bytes 772
  0.0 3.6 %copy-start.3 = (f32[4,64]{1,0:T(4,128)S(1)}, f32[4,64]{1,0:T(4,128)}, u32[]{:S(2)}) copy-start(f32[4,64]{1,0:T(4,128)} %param.14) | copy-start | bytes 3076
  0.0 4.5 %copy-start = (bf16[4,64,64]{2,1,0:T(8,128)(2,1)S(1)}, bf16[4,64,64]{2,1,0:T(8,128)(2,1)}, u32[]{:S(2)}) copy-start(bf16[4,64,64]{2,1,0:T(8,128)(2,1)} %param.13) | copy-start | bytes 98308
  0.0 5.2 %copy-start.2 = (s32[4,4,128]{2,1,0:T(4,128)S(1)}, s32[4,4,128]{2,1,0:T(4,128)}, u32[]{:S(2)}) copy-start(s32[4,4,128]{2,1,0:T(4,128)} %param.8) | copy-start | bytes 24580
  0.0 5.2 %copy-start.1 = (f32[4,4,128]{2,1,0:T(4,128)S(1)}, f32[4,4,128]{2,1,0:T(4,128)}, u32[]{:S(2)}) copy-start(f32[4,4,128]{2,1,0:T(4,128)} %param.9) | copy-start | bytes 24580

commit v13 on v12

--- a/solution.py
+++ b/solution.py
@@ -163,7 +163,12 @@
             plane = planes_ref[t // commit, row, pl.ds(t % commit, 1), :].astype(jnp.float32)
             value = plane * gain_ref[...] + bias_ref[...]
             value = value.astype(jnp.bfloat16).astype(jnp.float32)
-            feats[0, row, :, pl.ds(t * columns, columns)] = jnp.where(keep, value, 0.0)
+            feats[0, row, :, pl.ds(t * columns, columns)] = value
+
+        @pl.when(jnp.logical_not(keep))
+        def _():
+            feats[0, row] = jnp.zeros(feats.shape[2:], jnp.float32)
+
         return carry
 
     lax.fori_loop(0, extended, embed, 0)

time: 63.2 us -> 63.1 us (level)
  no operation moved by 1% of the time
where the time goes in v13:
time: 63.1 us; the launch traced here: 62.9 us
  Pallas kernels  57.1 us (90%)
  local copies, waits for them, and re-layouts  3.01 us (5%)
  other arithmetic  2.71 us (4%)
    pallas_call x1, Pallas kernels, run_network(): pl.pallas_call(functools.partial(network_kernel, rows, halo, layers), out...  37.8 us
    pallas_call x1, Pallas kernels, gather_window(): pl.pallas_call(functools.partial(exchange_kernel, axis_names, halo), out_...  19.2 us
    select_n x1, other arithmetic, run_network(): jnp.where(cancel[None, :, None, :], 0.0, taps)  2.59 us

profile of v13, /device:TPU:41, one launch (start us, length us, event | category | flops | bytes accessed | tf_op | source)
XLA Modules:
  0.0 62.9 jit_solution(16498798637098690901)
XLA Ops:
  0.0 0.0 copy-start.6
  0.0 0.0 copy-start.5
  0.0 0.0 copy-start.4
  0.0 0.0 copy-start.3
  0.0 0.0 copy-start
  0.0 0.0 copy-start.2
  0.0 0.0 copy-start.1
  0.1 0.1 and_or_fusion
  0.2 0.8 %copy.11 = f32[4,27,64]{2,1,0:T(8,128)S(1)} copy(f32[4,27,64]{2,0,1:T(4,128)} %bitcast.13) | data formatting | bytes 55296 | tf_op jit(solution)/shard_map/transpose | solution.py:241
  1.0 2.6 %broadcast_select_fusion.slabs_ref = f32[108,64,128]{2,1,0:T(8,128)} fusion(f32[108,64]{1,0:T(8,128)S(1)} %broadcast_in_dim.54, pred[108,128]{1,0:T(8,128)(4,1)S(1)} %broadcast_in_dim.51), kind=kLoop, calls=%fused_computation | loop fusion | flops 884736 | bytes 3580416 | tf_op jit(solution)/shard_map/jit(_where)/select_n | solution.py:242
  3.6 0.0 copy-done.6
  3.6 0.0 copy-done.5
  3.6 0.0 copy-done.4
  3.6 0.0 copy-done.3
  3.7 0.8 %broadcast_in_dim.60.small_ref = f32[7,64,128]{2,1,0:T(8,128)} broadcast(f32[7,64]{1,0:T(8,128)S(1)} %pad_maximum_fusion), dimensions={0,1} | broadcast | bytes 231168 | tf_op jit(solution)/shard_map/broadcast_in_dim | solution.py:246
  4.5 0.0 copy-done
  4.5 0.7 %copy.12 = bf16[4,64,64]{1,2,0:T(8,128)(2,1)} copy(bf16[4,64,64]{2,1,0:T(8,128)(2,1)S(1)} %copy-done) | data formatting | bytes 65536 | tf_op args[5]
  5.2 0.0 copy-done.2
  5.2 0.0 copy-done.1
  5.2 0.6 copy.14
  5.8 19.2 %shard_map.82.planes_ref = bf16[8,12,2,128]{3,2,1,0:T(2,128)(2,1)} custom-call(bf16[2,4,2,128]{3,2,1,0:T(2,128)(2,1)} %bitcast.15), custom_call_target="tpu_custom_call" | custom-call | tf_op jit(solution)/shard_map/pallas_call | solution.py:125
  25.1 37.8 %shard_map.83 = f32[16,4,128]{2,1,0:T(4,128)} custom-call(bf16[8,12,2,128]{3,2,1,0:T(2,128)(2,1)} %shard_map.82.planes_ref, f32[108,64,128]{2,1,0:T(8,128)} %broadcast_select_fusion.slabs_ref, f32[7,64,128]{2,1,0:T(8,128)} %broadcast_in_dim.60.small_ref, bf16[4,64,64]{2,1,0:T(8,128)(2,1)} %bitcast.12), custom_call_target="tpu_custom_call" | custom-call | tf_op jit(solution)/shard_map/pallas_call | solution.py:249
  (8 shorter events, 0.1 us)
Async XLA Ops:
  0.0 3.6 %copy-start.6 = (bf16[64]{0:T(256)(128)(2,1)S(1)}, bf16[64]{0:T(256)(128)(2,1)}, u32[]{:S(2)}) copy-start(bf16[64]{0:T(256)(128)(2,1)} %param.15) | copy-start | bytes 388
  0.0 3.6 %copy-start.5 = (f32[64]{0:T(128)S(1)}, f32[64]{0:T(128)}, u32[]{:S(2)}) copy-start(f32[64]{0:T(128)} %param.10) | copy-start | bytes 772
  0.0 3.6 %copy-start.4 = (f32[64]{0:T(128)S(1)}, f32[64]{0:T(128)}, u32[]{:S(2)}) copy-start(f32[64]{0:T(128)} %param.11) | copy-start | bytes 772
  0.0 3.6 %copy-start.3 = (f32[4,64]{1,0:T(4,128)S(1)}, f32[4,64]{1,0:T(4,128)}, u32[]{:S(2)}) copy-start(f32[4,64]{1,0:T(4,128)} %param.14) | copy-start | bytes 3076
  0.0 4.5 %copy-start = (bf16[4,64,64]{2,1,0:T(8,128)(2,1)S(1)}, bf16[4,64,64]{2,1,0:T(8,128)(2,1)}, u32[]{:S(2)}) copy-start(bf16[4,64,64]{2,1,0:T(8,128)(2,1)} %param.13) | copy-start | bytes 98308
  0.0 5.2 %copy-start.2 = (s32[4,4,128]{2,1,0:T(4,128)S(1)}, s32[4,4,128]{2,1,0:T(4,128)}, u32[]{:S(2)}) copy-start(s32[4,4,128]{2,1,0:T(4,128)} %param.8) | copy-start | bytes 24580
  0.0 5.2 %copy-start.1 = (f32[4,4,128]{2,1,0:T(4,128)S(1)}, f32[4,4,128]{2,1,0:T(4,128)}, u32[]{:S(2)}) copy-start(f32[4,4,128]{2,1,0:T(4,128)} %param.9) | copy-start | bytes 24580
